TPU v7x, 512 devices: a whole 4x4x16 slice. The times are simulated.
512 devices in a mesh: dp: 8 (over y, core), seq: 64 (over x, z).
Axes of the slice: x: 4, y: 4, z: 16, core: 2. Of those that a mesh axis runs over, the one named last changes fastest.
Arguments:
- queries: bfloat16 [16384, 3072], P('seq', 'dp'), may hold values from -6 to 6
- keys: bfloat16 [16384, 3072], P('seq', 'dp'), may hold values from -6 to 6
- values: bfloat16 [16384, 3072], P('seq', 'dp'), may hold values from -6 to 6
- out_grad: bfloat16 [16384, 3072], P('seq', 'dp'), may hold values from -6 to 6
- log_decay: float32 [16384, 24], P('seq', 'dp'), may hold values from -0.61 to 0
- norm_gain: float32 [3072], P('dp'), may hold values from 0.1 to 1.9
- doc_ids: int32 [128], P('seq'), may hold values from 0 to 3, never falling along the last dimension, each value on 1 to 64 neighbouring positions
Outputs:
- key_grad: bfloat16 [16384, 3072], P('seq', 'dp')
- value_grad: bfloat16 [16384, 3072], P('seq', 'dp')
- gain_grad: float32 [3072], P('dp')
Inputs may be any that keep to these rules, and one draw needn't show every extreme that they name: `doc_ids`: document numbers never fall along the sequence; every number from 0 to 3 occurs.
All inputs are finite; a program needn't handle non-finite values.
Results may differ from a plain program's by a relative error of at most 0.0052.
Values sent between devices are 32-bit elements; how exact they have to be, the bound alone decides.
A program may use at most 64 MiB of HBM per device.

v0:
```python
import jax
import jax.numpy as jnp
from jax import lax
from jax.sharding import PartitionSpec as P

C = 128


EPSILON = 1e-06


def from_behind(value, axis, steps):
    count = lax.axis_size(axis)
    leading, last = (max(0, -steps), min(count, count - steps))
    return lax.ppermute(value, axis, [(source, source + steps) for source in range(leading, last)])


def carried_in(part, axis, combine, identity, reverse):
    count = lax.axis_size(axis)
    place = lax.axis_index(axis)
    ahead = count - 1 - place if reverse else place
    gathered = jax.tree.map(lambda a: lax.all_gather(a, axis), part)
    state = jax.tree.map(lambda a, e: jnp.zeros_like(a) + jnp.asarray(e, a.dtype), part, identity)

    def one(lap, state):
        source = count - 1 - lap if reverse else lap
        return combine(
            state, jax.tree.map(lambda a: lax.dynamic_index_in_dim(a, source, 0, False), gathered)
        )

    return lax.fori_loop(0, ahead, one, state)


def combine_pairs(earlier, later):
    return (earlier[0] * later[0], later[0][..., None, None] * earlier[1] + later[1])


def far_grads(value_blocks, key_blocks, end_decay, later_grad):
    value_end = value_blocks.astype(jnp.float32) * end_decay[..., None]
    key_end = key_blocks.astype(jnp.float32) * end_decay[..., None]
    key_far = jnp.einsum("nshe,nhde->nshd", value_end, later_grad, precision=lax.Precision.HIGHEST)
    value_far = jnp.einsum("nshd,nhde->nshe", key_end, later_grad, precision=lax.Precision.HIGHEST)
    return (key_far, value_far)


def per_device(queries, keys, values, out_grad, log_decay, norm_gain, doc_ids):
    tokens = queries.shape[0]
    features = queries.shape[1]
    head_count = log_decay.shape[1]
    head_width = features // head_count
    all_features = features * lax.axis_size("dp")
    block_len = C
    nblocks = tokens // block_len
    block_shape = (nblocks, block_len, head_count, head_width)
    query_blocks = queries.reshape(block_shape)
    key_blocks = keys.reshape(block_shape)
    value_blocks = values.reshape(block_shape)
    cumulative = jnp.cumsum(log_decay.reshape(nblocks, block_len, head_count), axis=1)
    block_total = cumulative[:, -1, :]
    marked = from_behind(doc_ids[-1:] + 1, "seq", 1)
    before = marked - 1
    prev_ids = jnp.concatenate([before, doc_ids[:-1]])
    carried = (prev_ids == doc_ids).astype(jnp.float32)
    causal = (jnp.arange(block_len)[:, None] >= jnp.arange(block_len)[None, :]).astype(jnp.float32)
    log_gap = jnp.swapaxes(cumulative, 1, 2)
    decay_mask = jnp.exp(jnp.minimum(log_gap[:, :, :, None] - log_gap[:, :, None, :], 0.0)) * causal
    scores = jnp.einsum(
        "nthd,nshd->nhts", query_blocks, key_blocks, preferred_element_type=jnp.float32
    )
    weights = (scores * decay_mask).astype(jnp.bfloat16)
    local_out = jnp.einsum(
        "nhts,nshd->nthd", weights, value_blocks, preferred_element_type=jnp.float32
    )
    end_decay = jnp.exp(block_total[:, None, :] - cumulative)
    key_scaled = (key_blocks.astype(jnp.float32) * end_decay[..., None]).astype(jnp.bfloat16)
    update = jnp.einsum(
        "nshd,nshe->nhde", key_scaled, value_blocks, preferred_element_type=jnp.float32
    )
    factor = carried[:, None] * jnp.exp(block_total)

    def forward_step(carry_pair, block_item):
        acc_factor, acc_state = carry_pair
        blk_factor, blk_update = block_item
        nxt = (acc_factor * blk_factor, blk_factor[:, None, None] * acc_state + blk_update)
        return (nxt, (acc_factor, acc_state))

    identity = (
        jnp.ones((head_count,), jnp.float32),
        jnp.zeros((head_count, head_width, head_width), jnp.float32),
    )
    summary, (lead_factor, lead_state) = lax.scan(forward_step, identity, (factor, update))
    prefix = carried_in(summary, "seq", combine_pairs, identity, False)
    state_in = lead_factor[:, :, None, None] * prefix[1][None] + lead_state
    query_scaled = (
        query_blocks.astype(jnp.float32) * (jnp.exp(cumulative) * carried[:, None, None])[..., None]
    )
    far_out = jnp.einsum("nthd,nhde->nthe", query_scaled, state_in, precision=lax.Precision.HIGHEST)
    attention = (local_out + far_out).reshape(tokens, features)
    out_cot = out_grad.astype(jnp.float32)
    weighted = out_cot * norm_gain
    square_part = jnp.sum(attention * attention, axis=1)
    inner_part = jnp.sum(weighted * attention, axis=1)
    square_total, inner_total = lax.psum((square_part, inner_part), "dp")
    inverse = lax.rsqrt(square_total[:, None] / all_features + EPSILON)
    inner = inner_total[:, None] / all_features
    attn_grad = ((weighted - attention * inner * inverse * inverse) * inverse).astype(jnp.bfloat16)
    gain_part = jnp.sum(out_cot * attention * inverse, axis=0)
    grad_attn = attn_grad.reshape(block_shape)
    query_weighted = (query_blocks.astype(jnp.float32) * jnp.exp(cumulative)[..., None]).astype(
        jnp.bfloat16
    )
    back_term = jnp.einsum(
        "nthd,nthe->nhde", query_weighted, grad_attn, preferred_element_type=jnp.float32
    )
    back_term = back_term * carried[:, None, None, None]

    def backward_step(carry_pair, block_item):
        acc_factor, acc_term = carry_pair
        blk_factor, blk_term = block_item
        nxt = (acc_factor * blk_factor, blk_term + blk_factor[:, None, None] * acc_term)
        return (nxt, (acc_factor, acc_term))

    back_summary, (trail_factor, trail_term) = lax.scan(
        backward_step, identity, (factor, back_term), reverse=True
    )
    value_local = jnp.einsum(
        "nhts,nthd->nshd", weights, grad_attn, preferred_element_type=jnp.float32
    )
    grad_dot = jnp.einsum(
        "nthd,nshd->nhts", grad_attn, value_blocks, preferred_element_type=jnp.float32
    )
    grad_weights = (grad_dot * decay_mask).astype(jnp.bfloat16)
    key_local = jnp.einsum(
        "nhts,nthd->nshd", grad_weights, query_blocks, preferred_element_type=jnp.float32
    )
    suffix = carried_in(back_summary, "seq", combine_pairs, identity, True)
    later_grad = trail_factor[:, :, None, None] * suffix[1][None] + trail_term
    key_far, value_far = far_grads(value_blocks, key_blocks, end_decay, later_grad)
    gain_grad = lax.psum(gain_part, "seq")
    key_grad = (key_local + key_far).reshape(tokens, features).astype(jnp.bfloat16)
    value_grad = (value_local + value_far).reshape(tokens, features).astype(jnp.bfloat16)
    return (key_grad, value_grad, gain_grad)


def solution(mesh):
    placed = (
        P("seq", "dp"),
        P("seq", "dp"),
        P("seq", "dp"),
        P("seq", "dp"),
        P("seq", "dp"),
        P("dp"),
        P("seq"),
    )
    return jax.shard_map(
        per_device,
        mesh=mesh,
        in_specs=placed,
        out_specs=(P("seq", "dp"), P("seq", "dp"), P("dp")),
        check_vma=False,
    )
```

profile of v0, /device:TPU:1, one launch (start us, length us, event | category | flops | bytes accessed | tf_op | source)
XLA Modules:
  0.0 527.4 jit_solution(5625188076558059819)
XLA Ops:
  7.2 1.3 fusion.67
  9.2 5.1 collective-permute-start
  18.0 1.4 compare_convert_fusion
  22.3 1.1 copy.96
  23.3 1.3 dynamic-slice
  25.9 120.1 %all-reduce = f32[192]{0:T(256)S(1)} all-reduce(f32[192]{0:T(256)S(1)} %dynamic-update-slice), channel_id=2, replica_groups=mesh['dp'=8,'seq'=64] {'seq'}, use_global_device_ids=true, to_apply=%add | all-reduce | flops 192 | bytes 1536
  146.3 47.6 %all-gather.7.cloned.1.call-done = f32[192,128,128]{2,1,0:T(8,128)} async-done(((f32[3,128,128]{2,1,0:T(8,128)}), f32[192,128,128]{2,1,0:T(8,128)}) %all-gather.7.cloned.1.call-update) | async-done | bytes 12582928 | tf_op jit(solution)/shard_map/all_gather | solution.py:22
  195.5 15.1 %psum.22 = f32[256]{0:T(256)S(1)} all-reduce(f32[256]{0:T(256)S(1)} %bitcast.101), channel_id=1, replica_groups=mesh['dp'=8,'seq'=64] {'dp'}, use_global_device_ids=true, to_apply=%region_8.9 | all-reduce | flops 256 | bytes 2048 | tf_op jit(solution)/shard_map/psum | solution.py:103
  210.8 12.4 %psum.21 = f32[256]{0:T(256)S(1)} all-reduce(f32[256]{0:T(256)S(1)} %get-tuple-element.383), channel_id=1, replica_groups=mesh['dp'=8,'seq'=64] {'dp'}, use_global_device_ids=true, to_apply=%region_6.7 | all-reduce | flops 256 | bytes 2048 | tf_op jit(solution)/shard_map/psum | solution.py:103
  225.3 182.0 %all-reduce.2 = (f32[192]{0:T(256)S(1)}, f32[384]{0:T(512)}) all-reduce(f32[192]{0:T(256)S(1)} %dynamic-update-slice.1, f32[384]{0:T(512)S(1)} %get-tuple-element.382), channel_id=4, replica_groups=mesh['dp'=8,'seq'=64] {'seq'}, use_global_device_ids=true, to_apply=%add.1 | all-reduce | flops 576 | bytes 4608
  407.4 41.5 %all-gather.9.cloned.1.call-done = f32[192,128,128]{2,1,0:T(8,128)} async-done(((f32[3,128,128]{2,1,0:T(8,128)}), f32[192,128,128]{2,1,0:T(8,128)}) %all-gather.9.cloned.1.call-update) | async-done | bytes 12582928 | tf_op jit(solution)/shard_map/all_gather | solution.py:22
  448.9 67.8 %while.65 = (s32[]{:T(128)}, f32[3,128,128]{2,1,0:T(8,128)S(1)}, s32[]{:T(128)}, f32[64,3]{1,0:T(8,128)S(1)}, f32[64,3,128,128]{3,2,1,0:T(8,128)}, /*index=5*/s32[]{:T(128)}, s32[]{:T(128)}, s32[]{:T(128)}, s32[]{:T(128)}) while((s32[]{:T(128)}, f32[3,128,128]{2,1,0:T(8,128)S(1)}, s32[]{:T(128)}, f32[64,3]{1,0:T(8,128)S(1)}, ...), condition=%wide.region_12.13_spmd, body=%wide.region_11.12_spmd.sunk | while | flops 98310 | bytes 590007 | solution.py:31
  448.9 1.0 bitcast_add_fusion.9
  450.0 1.0 bitcast_add_fusion.9
  451.1 1.0 bitcast_add_fusion.9
  452.2 1.0 bitcast_add_fusion.9
  453.2 1.0 bitcast_add_fusion.9
  454.3 1.0 bitcast_add_fusion.9
  455.4 1.0 bitcast_add_fusion.9
  456.5 1.0 bitcast_add_fusion.9
  457.5 1.0 bitcast_add_fusion.9
  458.6 1.0 bitcast_add_fusion.9
  459.7 1.0 bitcast_add_fusion.9
  460.8 1.0 bitcast_add_fusion.9
  461.8 1.0 bitcast_add_fusion.9
  462.9 1.0 bitcast_add_fusion.9
  464.0 1.0 bitcast_add_fusion.9
  465.1 1.0 bitcast_add_fusion.9
  466.1 1.0 bitcast_add_fusion.9
  467.2 1.0 bitcast_add_fusion.9
  468.3 1.0 bitcast_add_fusion.9
  469.4 1.0 bitcast_add_fusion.9
  470.5 1.0 bitcast_add_fusion.9
  471.5 1.0 bitcast_add_fusion.9
  472.6 1.0 bitcast_add_fusion.9
  473.7 1.0 bitcast_add_fusion.9
  474.8 1.0 bitcast_add_fusion.9
  475.8 1.0 bitcast_add_fusion.9
  476.9 1.0 bitcast_add_fusion.9
  478.0 1.0 bitcast_add_fusion.9
  479.1 1.0 bitcast_add_fusion.9
  480.1 1.0 bitcast_add_fusion.9
  481.2 1.0 bitcast_add_fusion.9
  482.3 1.0 bitcast_add_fusion.9
  483.4 1.0 bitcast_add_fusion.9
  484.4 1.0 bitcast_add_fusion.9
  499.5 1.0 bitcast_add_fusion.9
  516.7 1.1 convolution_bitcast_fusion
  (167 shorter events, 43.6 us)
Async XLA Ops:
  7.2 203.4 %copy-start.2 = (f32[384]{0:T(512)S(1)}, f32[384]{0:T(512)}, u32[]{:S(2)}) copy-start(f32[384]{0:T(512)} %param.20) | copy-start | bytes 4612
  7.2 186.8 %all-gather.7.cloned.1.call-start = ((), (), s32[]{:S(2)}) async-start(), calls=%async_computation | async-start | bytes 12779520 | tf_op jit(solution)/shard_map/all_gather | solution.py:22
  9.2 8.1 %collective-permute-start = (s32[1]{0:T(128)}, s32[1]{0:T(128)}, u32[]{:S(2)}, u32[]{:S(2)}) collective-permute-start(s32[1]{0:T(128)} %add.103), channel_id=1, source_target_pairs={{0,1},{1,2},{2,3},{3,4},{4,5},{5,6},{6,7},{7,8},{8,9},{9,10},{10,1... | collective-permute-start | bytes 20 | tf_op jit(solution)/shard_map/ppermute | solution.py:15
  20.4 0.7 copy-start.1
  21.1 427.8 %all-gather.9.cloned.1.call-start = ((), (), s32[]{:S(2)}) async-start(), calls=%async_computation.1 | async-start | bytes 12779520 | tf_op jit(solution)/shard_map/all_gather | solution.py:22
  224.3 0.7 copy-start
Sparse Core Ops, SparseCore 0:
  21.2 172.6 all-gather.6
  225.2 223.6 all-gather.8
where the time goes:
time: 531 us; the launch traced here: 527 us
  blocking collectives  330 us (62%)
  waiting for transfers between devices  89.1 us (17%)
  other arithmetic  67.4 us (13%)
  between operations  16.3 us (3%)
  local copies, waits for them, and re-layouts  12.4 us (2%)
    unnamed x2, blocking collectives  302 us
    all_gather x2, waiting for transfers between devices, carried_in(): gathered = jax.tree.map(lambda a: lax.all_gather(a, axis), part)  89.1 us
    add x63, other arithmetic, combine_pairs(): later[0][..., None, None] * earlier[1] + later[1]  64.8 us
    psum x2, blocking collectives, per_device(): square_total, inner_total = lax.psum((square_part, inner_part), 'dp')  27.5 us
  transfers between devices with their start and end apart: 3, of which 2 were waited for; matrix products, arithmetic and copies ran while one was open for 1% of the time, Pallas kernels for 0%

commit v1 on v0

v1 whole, which is shorter than its diff:
```python
import jax
import jax.numpy as jnp
from jax import lax
from jax.experimental import pallas as pl
from jax.experimental.pallas import tpu as pltpu
from jax.sharding import PartitionSpec as P

C = 128
NZ = 16
EPSILON = 1e-06
MESH = pl.DeviceIdType.MESH
F32 = jnp.float32
BF16 = jnp.bfloat16


def dot(a, b, ca, cb, precision=None):
    return lax.dot_general(
        a, b, (((ca,), (cb,)), ((), ())), precision=precision, preferred_element_type=F32
    )


def split(x):
    high = x.astype(BF16)
    return high, (x - high.astype(F32)).astype(BF16)


def dot_split(high, low, b, cb):
    b_high, b_low = split(b)
    return dot(high, b_high, 1, cb) + (dot(high, b_low, 1, cb) + dot(low, b_high, 1, cb))


def kernel(
    heads,
    nx,
    ndp,
    q_hbm,
    k_hbm,
    v_hbm,
    o_hbm,
    log_hbm,
    gain_hbm,
    doc_hbm,
    kout_hbm,
    vout_hbm,
    gout_hbm,
    q_ref,
    k_ref,
    v_ref,
    o_ref,
    log_ref,
    gain_ref,
    doc_ref,
    kout,
    vout,
    gout,
    mask_ref,
    w_ref,
    u0_ref,
    qe_ref,
    qw_ref,
    ve_ref,
    ke_ref,
    part_ref,
    att_ref,
    ag_ref,
    bt1_ref,
    keyp_ref,
    valp_ref,
    info_s,
    info_r,
    u_s,
    u_r,
    pre_ref,
    x_s,
    x_r,
    a_s,
    a_r,
    st_s,
    st_r,
    b_s,
    b_r,
    bpre_ref,
    y_s,
    y_r,
    l_s,
    l_r,
    g_s,
    g_r,
    h_s,
    h_r,
    load_sem,
    store_sem,
    zs_sem,
    zr_sem,
    xs_sem,
    xr_sem,
    ds_sem,
    dr_sem,
):
    place = lax.axis_index("seq")
    me = lax.axis_index("dp")
    x = lax.div(place, NZ)
    z = lax.rem(place, NZ)
    rows = C // NZ
    tokens = 2 * C

    loads = [
        pltpu.make_async_copy(src, dst, load_sem.at[i])
        for i, (src, dst) in enumerate(
            (
                (log_hbm, log_ref),
                (doc_hbm, doc_ref),
                (k_hbm, k_ref),
                (v_hbm, v_ref),
                (q_hbm, q_ref),
                (o_hbm, o_ref),
                (gain_hbm, gain_ref),
            )
        )
    ]
    for load in loads:
        load.start()

    def each_z(run):
        def body(i, carry):
            half = lax.div(i + 1, 2)
            away = NZ // 2 + half * (1 - 2 * lax.rem(i, 2))
            run(lax.rem(z + away, NZ))
            return carry

        lax.fori_loop(0, NZ - 1, body, 0)

    def each_x(run):
        def body(i, carry):
            run(lax.rem(x + i, nx))
            return carry

        lax.fori_loop(1, nx, body, 0)

    def each_dp(run):
        def body(i, carry):
            run(lax.rem(me + i, ndp))
            return carry

        lax.fori_loop(1, ndp, body, 0)

    def z_copy(phase, src, dst, to, slot):
        return pltpu.make_async_remote_copy(
            src_ref=src,
            dst_ref=dst.at[slot],
            send_sem=zs_sem.at[phase, to],
            recv_sem=zr_sem.at[phase, slot],
            device_id={"seq": x * NZ + to},
            device_id_type=MESH,
        )

    def x_copy(phase, src, dst, to, slot):
        return pltpu.make_async_remote_copy(
            src_ref=src,
            dst_ref=dst.at[slot],
            send_sem=xs_sem.at[phase, to],
            recv_sem=xr_sem.at[phase, slot],
            device_id={"seq": to * NZ + z},
            device_id_type=MESH,
        )

    def d_copy(to, slot):
        return pltpu.make_async_remote_copy(
            src_ref=st_s,
            dst_ref=st_r.at[slot],
            send_sem=ds_sem.at[to],
            recv_sem=dr_sem.at[slot],
            device_id={"dp": to},
            device_id_type=MESH,
        )

    barrier = pltpu.get_barrier_semaphore()

    def greet(**where):
        pl.semaphore_signal(barrier, inc=1, device_id=where, device_id_type=MESH)

    each_z(lambda t: greet(seq=x * NZ + t))
    each_x(lambda t: greet(seq=t * NZ + z))
    each_dp(lambda t: greet(dp=t))

    for load in loads[:2]:
        load.wait()
    logs = jnp.concatenate(
        [log_ref[:, :C], log_ref[:, C:], jnp.zeros((8 - 2 * heads, C), F32)], axis=0
    )
    row_id = lax.broadcasted_iota(jnp.int32, (C, C), 0)
    col_id = lax.broadcasted_iota(jnp.int32, (C, C), 1)
    cum_rows = dot(logs, (row_id <= col_id).astype(F32), 1, 0, lax.Precision.HIGHEST)
    cum = cum_rows.T
    total = cum[C - 1 :, :]
    from_start = jnp.exp(cum)
    to_end = jnp.exp(total - cum)
    whole = jnp.exp(total)
    joined = jnp.where(doc_ref[0] == doc_ref[1], jnp.float32(1.0), jnp.float32(0.0))

    def at(table, block, head):
        r = block * heads + head
        return table[:, r : r + 1]

    def lanes(head):
        return slice(head * C, (head + 1) * C)

    for head in range(heads):
        info_s[:, lanes(head)] = jnp.broadcast_to(
            at(whole, 0, head) * (joined * at(whole, 1, head)), (1, C)
        )
    info_s[:, lanes(heads)] = jnp.full((1, C), doc_ref[0], jnp.int32).astype(F32)
    info_s[:, lanes(heads + 1)] = jnp.full((1, C), doc_ref[1], jnp.int32).astype(F32)

    for load in loads[2:4]:
        load.wait()
    for head in range(heads):
        updates = []
        for block in range(2):
            here = slice(block * C, (block + 1) * C)
            scaled = k_ref[here, lanes(head)].astype(F32) * at(to_end, block, head)
            updates.append(dot(scaled.astype(BF16), v_ref[here, lanes(head)], 0, 0))
        u0_ref[head] = updates[0]
        both = (joined * at(whole, 1, head)) * updates[0] + updates[1]
        u_s[:, head] = both.reshape(NZ, rows, C)

    pl.semaphore_wait(barrier, (NZ - 1) + (nx - 1) + (ndp - 1))
    each_z(lambda t: z_copy(0, info_s, info_r, t, z).start())
    each_z(lambda t: z_copy(1, u_s.at[t], u_r, t, z).start())
    info_r[z] = info_s[...]
    u_r[z] = u_s[z]

    for load in loads[4:]:
        load.wait()
    for head in range(heads):
        for block in range(2):
            here = slice(block * C, (block + 1) * C)
            r = block * heads + head
            gap = cum[:, r : r + 1] - cum_rows[r : r + 1, :]
            mask = jnp.where(row_id >= col_id, jnp.exp(jnp.minimum(gap, 0.0)), 0.0)
            mask_ref[r] = mask
            query = q_ref[here, lanes(head)]
            key = k_ref[here, lanes(head)]
            value = v_ref[here, lanes(head)]
            weights = (dot(query, key, 1, 1) * mask).astype(BF16)
            w_ref[r] = weights
            local = dot(weights, value, 1, 0)
            weighted = query.astype(F32) * at(from_start, block, head)
            qw_ref[r] = weighted.astype(BF16)
            if block == 1:
                high, low = split(weighted * joined)
                local = local + dot_split(high, low, u0_ref[head], 0)
                weighted = weighted * (joined * at(whole, 0, head))
            high, low = split(weighted)
            qe_ref[0, head, here] = high
            qe_ref[1, head, here] = low
            part_ref[here, lanes(head)] = local
            ending = at(to_end, block, head)
            if block == 0:
                ending = ending * (joined * at(whole, 1, head))
            high, low = split(value.astype(F32) * ending)
            ve_ref[0, head, here] = high
            ve_ref[1, head, here] = low
            high, low = split(key.astype(F32) * ending)
            ke_ref[0, head, here] = high
            ke_ref[1, head, here] = low

    each_z(lambda t: z_copy(0, info_s, info_r, t, t).wait_recv())

    def decay_of(t):
        return [
            jnp.broadcast_to(info_r[t, :, lanes(head)], (rows, C)) for head in range(heads)
        ]

    def first_doc(t):
        return info_r[t, :, lanes(heads)]

    def last_doc(t):
        return info_r[t, :, lanes(heads + 1)]

    def goes_on(later, earlier):
        return jnp.broadcast_to(jnp.where(later == earlier, 1.0, 0.0), (rows, C))

    each_z(lambda t: z_copy(1, u_s.at[t], u_r, t, t).wait_recv())
    state = [jnp.zeros((rows, C), F32)] * heads
    reach = [jnp.ones((rows, C), F32)] * heads
    for t in range(NZ):
        decay = decay_of(t)
        if t:
            keeps = goes_on(first_doc(t), last_doc(t - 1))
            state = [keeps * s for s in state]
            reach = [keeps * f for f in reach]
        for head in range(heads):
            pre_ref[0, t, head] = state[head]
            pre_ref[1, t, head] = reach[head]
        state = [decay[h] * state[h] + u_r[t, h] for h in range(heads)]
        reach = [decay[h] * reach[h] for h in range(heads)]
    for head in range(heads):
        x_s[head] = state[head]
        x_s[heads, head : head + 1] = reach[head][0:1]
    x_s[heads, heads : heads + 1] = first_doc(0)
    x_s[heads, heads + 1 : heads + 2] = last_doc(NZ - 1)
    each_x(lambda t: x_copy(0, x_s, x_r, t, x).start())
    x_r[x] = x_s[...]
    each_x(lambda t: x_copy(0, x_s, x_r, t, t).wait_recv())

    row_keeps = [None] + [
        goes_on(x_r[r, heads, heads : heads + 1], x_r[r - 1, heads, heads + 1 : heads + 2])
        for r in range(1, nx)
    ]
    row_reach = [
        [jnp.broadcast_to(x_r[r, heads, h : h + 1], (rows, C)) for h in range(heads)]
        for r in range(nx)
    ]
    entering = [jnp.zeros((rows, C), F32)] * heads
    chosen = entering
    for r in range(1, nx):
        entering = [
            row_keeps[r] * (x_r[r - 1, h] + row_reach[r - 1][h] * entering[h])
            for h in range(heads)
        ]
        chosen = [jnp.where(x == r, entering[h], chosen[h]) for h in range(heads)]
    for t in range(NZ):
        for head in range(heads):
            a_s[t, head] = pre_ref[0, t, head] + pre_ref[1, t, head] * chosen[head]
    each_z(lambda t: z_copy(2, a_s.at[t], a_r, t, z).start())
    a_r[z] = a_s[z]
    each_z(lambda t: z_copy(2, a_s.at[t], a_r, t, t).wait_recv())

    squares = jnp.zeros((tokens, C), F32)
    inners = jnp.zeros((tokens, C), F32)
    for head in range(heads):
        came = a_r[:, head].reshape(C, C)
        attention = part_ref[:, lanes(head)] + dot_split(qe_ref[0, head], qe_ref[1, head], came, 0)
        att_ref[:, lanes(head)] = attention
        wanted = o_ref[:, lanes(head)].astype(F32) * gain_ref[:, lanes(head)]
        squares = squares + attention * attention
        inners = inners + wanted * attention
    lane = lax.broadcasted_iota(jnp.int32, (tokens, C), 1)
    stats = jnp.where(
        lane == 0,
        jnp.sum(squares, axis=1, keepdims=True),
        jnp.sum(inners, axis=1, keepdims=True),
    ).T
    st_s[...] = stats[0:2]
    each_dp(lambda t: d_copy(t, me).start())
    st_r[me] = st_s[...]
    each_dp(lambda t: d_copy(t, t).wait_recv())
    sums = st_r[0]
    for r in range(1, ndp):
        sums = sums + st_r[r]
    means = sums / (ndp * heads * C)
    inverse = lax.rsqrt(means[0:1] + EPSILON)
    bend = means[1:2] * inverse * inverse
    side = lax.broadcasted_iota(jnp.int32, (8, tokens), 0)
    columns = jnp.where(side == 0, inverse, bend).T
    inverse = columns[:, 0:1]
    bend = columns[:, 1:2]

    for head in range(heads):
        attention = att_ref[:, lanes(head)]
        out_cot = o_ref[:, lanes(head)].astype(F32)
        wanted = out_cot * gain_ref[:, lanes(head)]
        grad = ((wanted - attention * bend) * inverse).astype(BF16)
        ag_ref[:, lanes(head)] = grad
        back = [
            dot(qw_ref[b * heads + head], grad[b * C : (b + 1) * C], 0, 0) for b in range(2)
        ]
        back_next = joined * back[1]
        bt1_ref[head] = back_next
        b_s[:, head] = (back[0] + at(whole, 0, head) * back_next).reshape(NZ, rows, C)
    each_z(lambda t: z_copy(3, b_s.at[t], b_r, t, z).start())
    b_r[z] = b_s[z]

    for head in range(heads):
        attention = att_ref[:, lanes(head)]
        out_cot = o_ref[:, lanes(head)].astype(F32)
        g_s[:, lanes(head)] = jnp.sum(out_cot * attention * inverse, axis=0, keepdims=True)
    each_z(lambda t: z_copy(4, g_s, g_r, t, z).start())
    g_r[z] = g_s[...]

    for head in range(heads):
        for block in range(2):
            here = slice(block * C, (block + 1) * C)
            r = block * heads + head
            grad = ag_ref[here, lanes(head)]
            value = v_ref[here, lanes(head)]
            key = k_ref[here, lanes(head)]
            value_part = dot(w_ref[r], grad, 0, 0)
            grad_weights = (dot(grad, value, 1, 1) * mask_ref[r]).astype(BF16)
            key_part = dot(grad_weights, q_ref[here, lanes(head)], 0, 0)
            if block == 0:
                ending = at(to_end, 0, head)
                high, low = split(value.astype(F32) * ending)
                key_part = key_part + dot_split(high, low, bt1_ref[head], 1)
                high, low = split(key.astype(F32) * ending)
                value_part = value_part + dot_split(high, low, bt1_ref[head], 0)
            keyp_ref[here, lanes(head)] = key_part
            valp_ref[here, lanes(head)] = value_part

    each_z(lambda t: z_copy(3, b_s.at[t], b_r, t, t).wait_recv())
    state = [jnp.zeros((rows, C), F32)] * heads
    reach = [jnp.ones((rows, C), F32)] * heads
    for t in range(NZ - 1, -1, -1):
        decay = decay_of(t)
        for head in range(heads):
            bpre_ref[0, t, head] = state[head]
            bpre_ref[1, t, head] = reach[head]
        state = [decay[h] * state[h] + b_r[t, h] for h in range(heads)]
        reach = [decay[h] * reach[h] for h in range(heads)]
        if t:
            keeps = goes_on(first_doc(t), last_doc(t - 1))
            state = [keeps * s for s in state]
            reach = [keeps * f for f in reach]
    for head in range(heads):
        y_s[head] = state[head]
    each_x(lambda t: x_copy(1, y_s, y_r, t, x).start())
    y_r[x] = y_s[...]

    each_z(lambda t: z_copy(4, g_s, g_r, t, t).wait_recv())
    row_gain = g_r[0]
    for t in range(1, NZ):
        row_gain = row_gain + g_r[t]
    h_s[...] = row_gain
    each_x(lambda t: x_copy(2, h_s, h_r, t, x).start())
    h_r[x] = h_s[...]

    each_x(lambda t: x_copy(1, y_s, y_r, t, t).wait_recv())
    entering = [jnp.zeros((rows, C), F32)] * heads
    chosen = entering
    for r in range(nx - 2, -1, -1):
        entering = [
            row_keeps[r + 1] * (y_r[r + 1, h] + row_reach[r + 1][h] * entering[h])
            for h in range(heads)
        ]
        chosen = [jnp.where(x == r, entering[h], chosen[h]) for h in range(heads)]
    for t in range(NZ):
        for head in range(heads):
            l_s[t, head] = bpre_ref[0, t, head] + bpre_ref[1, t, head] * chosen[head]
    each_z(lambda t: z_copy(5, l_s.at[t], l_r, t, z).start())
    l_r[z] = l_s[z]

    each_x(lambda t: x_copy(2, h_s, h_r, t, t).wait_recv())
    gain = h_r[0]
    for r in range(1, nx):
        gain = gain + h_r[r]
    gout[...] = gain
    stores = [
        pltpu.make_async_copy(src, dst, store_sem.at[i])
        for i, (src, dst) in enumerate(((kout, kout_hbm), (vout, vout_hbm), (gout, gout_hbm)))
    ]
    stores[2].start()

    each_z(lambda t: z_copy(5, l_s.at[t], l_r, t, t).wait_recv())
    for head in range(heads):
        came = l_r[:, head].reshape(C, C)
        far = dot_split(ve_ref[0, head], ve_ref[1, head], came, 1)
        kout[:, lanes(head)] = (keyp_ref[:, lanes(head)] + far).astype(BF16)
        far = dot_split(ke_ref[0, head], ke_ref[1, head], came, 0)
        vout[:, lanes(head)] = (valp_ref[:, lanes(head)] + far).astype(BF16)
    stores[0].start()
    stores[1].start()

    each_z(lambda t: z_copy(0, info_s, info_r, t, t).wait_send())
    each_z(lambda t: z_copy(1, u_s.at[t], u_r, t, t).wait_send())
    each_z(lambda t: z_copy(2, a_s.at[t], a_r, t, t).wait_send())
    each_z(lambda t: z_copy(3, b_s.at[t], b_r, t, t).wait_send())
    each_z(lambda t: z_copy(4, g_s, g_r, t, t).wait_send())
    each_z(lambda t: z_copy(5, l_s.at[t], l_r, t, t).wait_send())
    each_x(lambda t: x_copy(0, x_s, x_r, t, t).wait_send())
    each_x(lambda t: x_copy(1, y_s, y_r, t, t).wait_send())
    each_x(lambda t: x_copy(2, h_s, h_r, t, t).wait_send())
    each_dp(lambda t: d_copy(t, t).wait_send())
    for store in stores:
        store.wait()


def per_device(queries, keys, values, out_grad, log_decay, norm_gain, doc_ids):
    tokens, features = queries.shape
    heads = log_decay.shape[1]
    ndp = lax.axis_size("dp")
    nx = lax.axis_size("seq") // NZ
    rows = C // NZ
    wide = (tokens, features)
    squares = (2 * heads, C, C)
    table = (NZ, heads, rows, C)
    anywhere = pl.BlockSpec(memory_space=pl.ANY)
    scratch = [
        pltpu.VMEM(wide, BF16),
        pltpu.VMEM(wide, BF16),
        pltpu.VMEM(wide, BF16),
        pltpu.VMEM(wide, BF16),
        pltpu.VMEM((heads, tokens), F32),
        pltpu.VMEM((1, features), F32),
        pltpu.SMEM((2,), jnp.int32),
        pltpu.VMEM(wide, BF16),
        pltpu.VMEM(wide, BF16),
        pltpu.VMEM((1, features), F32),
        pltpu.VMEM(squares, F32),
        pltpu.VMEM(squares, BF16),
        pltpu.VMEM((heads, C, C), F32),
        pltpu.VMEM((2, heads, tokens, C), BF16),
        pltpu.VMEM(squares, BF16),
        pltpu.VMEM((2, heads, tokens, C), BF16),
        pltpu.VMEM((2, heads, tokens, C), BF16),
        pltpu.VMEM(wide, F32),
        pltpu.VMEM(wide, F32),
        pltpu.VMEM(wide, BF16),
        pltpu.VMEM((heads, C, C), F32),
        pltpu.VMEM(wide, F32),
        pltpu.VMEM(wide, F32),
        pltpu.VMEM((1, (heads + 2) * C), F32),
        pltpu.VMEM((NZ, 1, (heads + 2) * C), F32),
        pltpu.VMEM(table, F32),
        pltpu.VMEM(table, F32),
        pltpu.VMEM((2,) + table, F32),
        pltpu.VMEM((heads + 1, rows, C), F32),
        pltpu.VMEM((nx, heads + 1, rows, C), F32),
        pltpu.VMEM(table, F32),
        pltpu.VMEM(table, F32),
        pltpu.VMEM((2, tokens), F32),
        pltpu.VMEM((ndp, 2, tokens), F32),
        pltpu.VMEM(table, F32),
        pltpu.VMEM(table, F32),
        pltpu.VMEM((2,) + table, F32),
        pltpu.VMEM((heads, rows, C), F32),
        pltpu.VMEM((nx, heads, rows, C), F32),
        pltpu.VMEM(table, F32),
        pltpu.VMEM(table, F32),
        pltpu.VMEM((1, features), F32),
        pltpu.VMEM((NZ, 1, features), F32),
        pltpu.VMEM((1, features), F32),
        pltpu.VMEM((nx, 1, features), F32),
        pltpu.SemaphoreType.DMA((7,)),
        pltpu.SemaphoreType.DMA((3,)),
        pltpu.SemaphoreType.DMA((6, NZ)),
        pltpu.SemaphoreType.DMA((6, NZ)),
        pltpu.SemaphoreType.DMA((3, nx)),
        pltpu.SemaphoreType.DMA((3, nx)),
        pltpu.SemaphoreType.DMA((ndp,)),
        pltpu.SemaphoreType.DMA((ndp,)),
    ]

    def body(*refs):
        kernel(heads, nx, ndp, *refs)

    key_grad, value_grad, gain_grad = pl.pallas_call(
        body,
        out_shape=(
            jax.ShapeDtypeStruct(wide, BF16),
            jax.ShapeDtypeStruct(wide, BF16),
            jax.ShapeDtypeStruct((1, features), F32),
        ),
        in_specs=[anywhere] * 7,
        out_specs=(anywhere, anywhere, anywhere),
        scratch_shapes=scratch,
        compiler_params=pltpu.CompilerParams(collective_id=0, has_side_effects=True),
        name="attention_core",
    )(
        queries,
        keys,
        values,
        out_grad,
        log_decay.T,
        norm_gain.reshape(1, features),
        doc_ids,
    )
    return key_grad, value_grad, gain_grad.reshape(features)


def solution(mesh):
    placed = (
        P("seq", "dp"),
        P("seq", "dp"),
        P("seq", "dp"),
        P("seq", "dp"),
        P("seq", "dp"),
        P("dp"),
        P("seq"),
    )
    return jax.shard_map(
        per_device,
        mesh=mesh,
        in_specs=placed,
        out_specs=(P("seq", "dp"), P("seq", "dp"), P("dp")),
        check_vma=False,
    )
```

time: 531 us -> 83.4 us (0.16)
  blocking collectives: 330 us -> 0 us
  waiting for transfers between devices: 89.1 us -> 0 us
  Pallas kernels: 0 us -> 77.7 us
  other arithmetic: 67.4 us -> 0.6 us
  between operations: 16.3 us -> 0.65 us
  local copies, waits for them, and re-layouts: 12.4 us -> 4.23 us
    unnamed x2 -> x0, blocking collectives: 302 us -> none
    all_gather x2 -> x0, waiting for transfers between devices: 89.1 us -> none  [carried_in(): gathered = jax.tree.map(lambda a: lax.all_gather(a, axis), part)]
    pallas_call x0 -> x1, Pallas kernels: none -> 77.7 us  [per_device(): pl.pallas_call(body, out_shape=(jax.ShapeDtypeStruct(wide, BF16), jax.Sha...]
    add x67 -> x0, other arithmetic: 65.2 us -> none  [the longest x63 64.8 us: combine_pairs(): later[0][..., None, None] * earlier[1] + later[1]]
    psum x2 -> x0, blocking collectives: 27.5 us -> none  [per_device(): square_total, inner_total = lax.psum((square_part, inner_part), 'dp')]
  transfers between devices with their start and end apart: 3 -> 0, of which waited for: 2 -> 0; matrix products, arithmetic and copies ran while one was open for 1% -> 0% of each run, Pallas kernels for 0% -> 0%
where the time goes in v1:
time: 83.4 us; the launch traced here: 83.2 us
  Pallas kernels  77.7 us (93%)
  local copies, waits for them, and re-layouts  4.23 us (5%)
    pallas_call x1, Pallas kernels, per_device(): pl.pallas_call(body, out_shape=(jax.ShapeDtypeStruct(wide, BF16), jax.Sha...  77.7 us
    unnamed x6, local copies, waits for them, and re-layouts  2.99 us

profile of v1, /device:TPU:1, one launch (start us, length us, event | category | flops | bytes accessed | tf_op | source)
XLA Modules:
  0.0 83.2 jit_solution(2761264682329811511)
XLA Ops:
  0.6 1.2 %reshape.12.refs_5_ = f32[1,384]{1,0:T(1,128)} reshape(f32[384]{0:T(512)} %param.12) | data formatting | bytes 3072 | tf_op jit(solution)/shard_map/reshape | solution.py:565
  1.9 77.7 %attention_core.1 = (bf16[256,384]{1,0:T(8,128)(2,1)}, bf16[256,384]{1,0:T(8,128)(2,1)}, f32[1,384]{1,0:T(1,128)}) custom-call(bf16[256,384]{1,0:T(8,128)(2,1)} %refs_0_.1, bf16[256,384]{1,0:T(8,128)(2,1)} %refs_1_.1, bf16[256,384]{1,0:T(8,128)(2,1)} %refs_2_.1, bf16[256,384]{1,0:T(8,128)(2,1)} %refs_3_.1, f32[3,256]{1,0:T(4,128)} %bitcast.1, ...), custom_call_target="tpu_custom_call" | custom-call | tf_op jit(solution)/shard_map/attention_core/pallas_call | solution.py:547
  79.6 0.0 copy-start.1
  79.6 0.6 copy-done.1
  80.3 0.6 reduce
  80.9 0.0 copy-start
  80.9 1.7 %copy.12 = bf16[256,384]{1,0:T(8,128)(2,1)} copy(bf16[256,384]{1,0:T(8,128)(2,1)} %get-tuple-element.12) | data formatting | bytes 393216
  82.5 0.0 copy-done
  82.5 0.7 copy.13
Async XLA Ops:
  79.6 0.7 copy-start.1
  80.9 1.7 %copy-start = (bf16[256,384]{1,0:T(8,128)(2,1)S(1)}, bf16[256,384]{1,0:T(8,128)(2,1)}, u32[]{:S(2)}) copy-start(bf16[256,384]{1,0:T(8,128)(2,1)} %get-tuple-element.13) | copy-start | bytes 589828

commit v2 on v0

v2 whole, which is shorter than its diff:
```python
from typing import Any, NamedTuple

import jax
import jax.numpy as jnp
from jax import lax
from jax.experimental import pallas as pl
from jax.experimental.pallas import tpu as pltpu
from jax.sharding import PartitionSpec as P

C = 128
NZ = 16
EPSILON = 1e-06
MESH = pl.DeviceIdType.MESH
F32 = jnp.float32
BF16 = jnp.bfloat16


def dot(a, b, ca, cb, precision=None):
    return lax.dot_general(
        a, b, (((ca,), (cb,)), ((), ())), precision=precision, preferred_element_type=F32
    )


def split(x):
    high = x.astype(BF16)
    return high, (x - high.astype(F32)).astype(BF16)


def dot_split(high, low, b, cb):
    b_high, b_low = split(b)
    return dot(high, b_high, 1, cb) + (dot(high, b_low, 1, cb) + dot(low, b_high, 1, cb))


class Scan(NamedTuple):
    up_s: Any
    up_r: Any
    pre: Any
    x_s: Any
    x_r: Any
    down_s: Any
    down_r: Any


def groups_of(heads):
    return ((0,), tuple(range(1, heads)))


def kernel(heads, nx, ndp, ins, outs, local, info, scans, norm, gains, sems):
    q_hbm, k_hbm, v_hbm, o_hbm, log_hbm, gain_hbm, doc_hbm = ins
    kout, vout, gout = outs
    (
        (q_ref, k_ref, v_ref, o_ref, log_ref, gain_ref, doc_ref),
        (mask_ref, w_ref, u0_ref, qe_ref, qw_ref, ve_ref, ke_ref),
        (part_ref, att_ref, ag_ref, bt1_ref, keyp_ref, valp_ref),
    ) = local
    info_s, info_r, keep_ref, step_ref, reach_ref, end_ref, row_s, row_r = info
    st_s, st_r = norm
    g_s, g_r, h_s, h_r = gains
    load_sem, zs_sem, zr_sem, xs_sem, xr_sem, ds_sem, dr_sem = sems
    groups = groups_of(heads)
    place = lax.axis_index("seq")
    me = lax.axis_index("dp")
    x = lax.div(place, NZ)
    z = lax.rem(place, NZ)
    rows = C // NZ
    tokens = 2 * C

    loads = [
        pltpu.make_async_copy(src, dst, load_sem.at[i])
        for i, (src, dst) in enumerate(
            (
                (log_hbm, log_ref),
                (doc_hbm, doc_ref),
                (k_hbm, k_ref),
                (v_hbm, v_ref),
                (q_hbm, q_ref),
                (o_hbm, o_ref),
                (gain_hbm, gain_ref.at[0]),
            )
        )
    ]
    for load in loads:
        load.start()

    def each_z(run):
        def body(i, carry):
            half = lax.div(i + 1, 2)
            away = NZ // 2 + half * (1 - 2 * lax.rem(i, 2))
            run(lax.rem(z + away, NZ))
            return carry

        lax.fori_loop(0, NZ - 1, body, 0)

    def each_x(run):
        def body(i, carry):
            run(lax.rem(x + i, nx))
            return carry

        lax.fori_loop(1, nx, body, 0)

    def each_dp(run):
        def body(i, carry):
            run(lax.rem(me + i, ndp))
            return carry

        lax.fori_loop(1, ndp, body, 0)

    sent = []

    def exchange(each, where, mine, count, source, slots, send_sem, recv_sem):
        def start(t):
            pltpu.make_async_remote_copy(
                src_ref=source(t),
                dst_ref=slots.at[mine],
                send_sem=send_sem,
                recv_sem=recv_sem,
                device_id=where(t),
                device_id_type=MESH,
            ).start()

        each(start)
        slots[mine] = source(mine)[...]
        others = slots.at[pl.ds(0, count - 1)]
        whole = pltpu.make_async_remote_copy(
            src_ref=others,
            dst_ref=others,
            send_sem=send_sem,
            recv_sem=recv_sem,
            device_id=where(mine),
            device_id_type=MESH,
        )
        sent.append(whole)
        return whole.wait_recv

    def over_z(phase, source, slots):
        return exchange(
            each_z,
            lambda t: {"seq": x * NZ + t},
            z,
            NZ,
            source,
            slots,
            zs_sem.at[phase],
            zr_sem.at[phase],
        )

    def over_x(phase, source, slots):
        return exchange(
            each_x,
            lambda t: {"seq": t * NZ + z},
            x,
            nx,
            lambda t: source,
            slots,
            xs_sem.at[phase],
            xr_sem.at[phase],
        )

    barrier = pltpu.get_barrier_semaphore()

    def greet(**where):
        pl.semaphore_signal(barrier, inc=1, device_id=where, device_id_type=MESH)

    each_z(lambda t: greet(seq=x * NZ + t))
    each_x(lambda t: greet(seq=t * NZ + z))
    each_dp(lambda t: greet(dp=t))

    for load in loads[:2]:
        load.wait()
    logs = jnp.concatenate(
        [log_ref[:, :C], log_ref[:, C:], jnp.zeros((8 - 2 * heads, C), F32)], axis=0
    )
    row_id = lax.broadcasted_iota(jnp.int32, (C, C), 0)
    col_id = lax.broadcasted_iota(jnp.int32, (C, C), 1)
    cum_rows = dot(logs, (row_id <= col_id).astype(F32), 1, 0, lax.Precision.HIGHEST)
    cum = cum_rows.T
    total = cum[C - 1 :, :]
    from_start = jnp.exp(cum)
    to_end = jnp.exp(total - cum)
    whole = jnp.exp(total)
    joined = jnp.where(doc_ref[0] == doc_ref[1], jnp.float32(1.0), jnp.float32(0.0))

    def at(table, block, head):
        r = block * heads + head
        return table[:, r : r + 1]

    def lanes(head):
        return slice(head * C, (head + 1) * C)

    lane = lax.broadcasted_iota(jnp.int32, (1, C), 1)
    line = jnp.zeros((1, C), F32)
    for head in range(heads):
        line = jnp.where(
            lane == head, at(whole, 0, head) * (joined * at(whole, 1, head)), line
        )
    for i in range(2):
        document = jnp.full((1, C), doc_ref[i], jnp.int32).astype(F32)
        line = jnp.where(lane == heads + i, document, line)
    info_s[...] = line

    for load in loads[2:4]:
        load.wait()
    for group, scan in zip(groups, scans[0]):
        for i, head in enumerate(group):
            updates = []
            for block in range(2):
                here = slice(block * C, (block + 1) * C)
                scaled = k_ref[here, lanes(head)].astype(F32) * at(to_end, block, head)
                updates.append(dot(scaled.astype(BF16), v_ref[here, lanes(head)], 0, 0))
            u0_ref[head] = updates[0]
            both = (joined * at(whole, 1, head)) * updates[0] + updates[1]
            scan.up_s[:, i] = both.reshape(NZ, rows, C)

    pl.semaphore_wait(barrier, (NZ - 1) + (nx - 1) + (ndp - 1))
    info_wait = over_z(0, lambda t: info_s, info_r)
    up_waits = [
        over_z(1 + g, lambda t, scan=scan: scan.up_s.at[t], scan.up_r)
        for g, scan in enumerate(scans[0])
    ]

    info_wait()

    def tile(line, i):
        return jnp.broadcast_to(line[:, i : i + 1], (rows, C))

    def goes_on(later, earlier):
        return jnp.where(
            later[:, heads : heads + 1] == earlier[:, heads + 1 : heads + 2], 1.0, 0.0
        )

    line = info_r[0]
    reach = jnp.ones((1, C), F32)
    for t in range(NZ):
        if t:
            earlier, line = line, info_r[t]
            keeps = goes_on(line, earlier)
            keep_ref[t] = jnp.broadcast_to(keeps, (rows, C))
            for head in range(heads):
                step_ref[0, t, head] = tile(keeps * earlier, head)
                step_ref[1, t, head] = tile(keeps * line, head)
            reach = reach * (keeps * earlier)
        for head in range(heads):
            reach_ref[0, t, head] = tile(reach, head)
    first, last = info_r[0], info_r[NZ - 1]
    row_s[...] = jnp.where(
        lane < heads, reach * last, jnp.where(lane == heads, first, last)
    )
    row_wait = over_x(0, row_s, row_r)
    for head in range(heads):
        end_ref[0, head] = tile(last, head)
        end_ref[1, head] = tile(first, head)
    reach = jnp.ones((1, C), F32)
    for t in range(NZ - 1, -1, -1):
        for head in range(heads):
            reach_ref[1, t, head] = tile(reach, head)
        if t:
            reach = reach * (goes_on(info_r[t], info_r[t - 1]) * info_r[t])

    for load in loads[4:]:
        load.wait()
    for head in range(heads):
        for block in range(2):
            here = slice(block * C, (block + 1) * C)
            r = block * heads + head
            gap = cum[:, r : r + 1] - cum_rows[r : r + 1, :]
            mask = jnp.where(row_id >= col_id, jnp.exp(jnp.minimum(gap, 0.0)), 0.0)
            mask_ref[r] = mask
            query = q_ref[here, lanes(head)]
            key = k_ref[here, lanes(head)]
            value = v_ref[here, lanes(head)]
            weights = (dot(query, key, 1, 1) * mask).astype(BF16)
            w_ref[r] = weights
            near = dot(weights, value, 1, 0)
            weighted = query.astype(F32) * at(from_start, block, head)
            qw_ref[r] = weighted.astype(BF16)
            if block == 1:
                high, low = split(weighted * joined)
                near = near + dot_split(high, low, u0_ref[head], 0)
                weighted = weighted * (joined * at(whole, 0, head))
            high, low = split(weighted)
            qe_ref[0, head, here] = high
            qe_ref[1, head, here] = low
            part_ref[here, lanes(head)] = near
            ending = at(to_end, block, head)
            if block == 0:
                ending = ending * (joined * at(whole, 1, head))
            high, low = split(value.astype(F32) * ending)
            ve_ref[0, head, here] = high
            ve_ref[1, head, here] = low
            high, low = split(key.astype(F32) * ending)
            ke_ref[0, head, here] = high
            ke_ref[1, head, here] = low
    row_wait()
    row_lines = [row_r[r] for r in range(nx)]

    def scan_row(back, scan, group):
        count = len(group)
        state = [jnp.zeros((rows, C), F32)] * count
        order = range(NZ - 1, -1, -1) if back else range(NZ)
        for t in order:
            for i in range(count):
                scan.pre[t, i] = state[i]
            if t != order[-1]:
                link = t if back else t + 1
                state = [
                    step_ref[back, link, head] * state[i] + keep_ref[link] * scan.up_r[t, i]
                    for i, head in enumerate(group)
                ]
            else:
                for i, head in enumerate(group):
                    scan.x_s[i] = end_ref[back, head] * state[i] + scan.up_r[t, i]

    def scan_rows(back, scan, group):
        count = len(group)
        entering = [jnp.zeros((rows, C), F32)] * count
        chosen = entering
        for r in range(nx - 2, -1, -1) if back else range(1, nx):
            other = r + 1 if back else r - 1
            keeps = goes_on(row_lines[max(r, other)], row_lines[min(r, other)])
            entering = [
                jnp.broadcast_to(keeps, (rows, C)) * scan.x_r[other, i]
                + tile(keeps * row_lines[other], head) * entering[i]
                for i, head in enumerate(group)
            ]
            chosen = [jnp.where(x == r, entering[i], chosen[i]) for i in range(count)]
        for t in range(NZ):
            for i, head in enumerate(group):
                scan.down_s[t, i] = scan.pre[t, i] + reach_ref[back, t, head] * chosen[i]

    def scan_all(back, up_waits):
        base = 1 + back * 2 * len(groups)
        x_waits, down_waits = [], []
        for g, (group, scan) in enumerate(zip(groups, scans[back])):
            up_waits[g]()
            scan_row(back, scan, group)
            x_waits.append(over_x(1 + back * len(groups) + g, scan.x_s, scan.x_r))
        for g, (group, scan) in enumerate(zip(groups, scans[back])):
            x_waits[g]()
            scan_rows(back, scan, group)
            down_waits.append(
                over_z(
                    base + len(groups) + g, lambda t, scan=scan: scan.down_s.at[t], scan.down_r
                )
            )
        return down_waits

    down_waits = scan_all(0, up_waits)

    squares = jnp.zeros((tokens, C), F32)
    inners = jnp.zeros((tokens, C), F32)
    for group, scan, arrived in zip(groups, scans[0], down_waits):
        arrived()
        for i, head in enumerate(group):
            came = scan.down_r[:, i].reshape(C, C)
            far = dot_split(qe_ref[0, head], qe_ref[1, head], came, 0)
            attention = part_ref[:, lanes(head)] + far
            att_ref[:, lanes(head)] = attention
            wanted = o_ref[:, lanes(head)].astype(F32) * gain_ref[:, lanes(head)]
            squares = squares + attention * attention
            inners = inners + wanted * attention
    lane = lax.broadcasted_iota(jnp.int32, (tokens, C), 1)
    stats = jnp.where(
        lane == 0,
        jnp.sum(squares, axis=1, keepdims=True),
        jnp.sum(inners, axis=1, keepdims=True),
    ).T
    st_s[...] = stats[0:2]
    exchange(each_dp, lambda t: {"dp": t}, me, ndp, lambda t: st_s, st_r, ds_sem, dr_sem)()
    sums = st_r[0]
    for r in range(1, ndp):
        sums = sums + st_r[r]
    means = sums / (ndp * heads * C)
    inverse = lax.rsqrt(means[0:1] + EPSILON)
    bend = means[1:2] * inverse * inverse
    side = lax.broadcasted_iota(jnp.int32, (8, tokens), 0)
    columns = jnp.where(side == 0, inverse, bend).T
    inverse = columns[:, 0:1]
    bend = columns[:, 1:2]

    up_waits = []
    for g, (group, scan) in enumerate(zip(groups, scans[1])):
        for i, head in enumerate(group):
            attention = att_ref[:, lanes(head)]
            wanted = o_ref[:, lanes(head)].astype(F32) * gain_ref[:, lanes(head)]
            grad = ((wanted - attention * bend) * inverse).astype(BF16)
            ag_ref[:, lanes(head)] = grad
            back = [
                dot(qw_ref[b * heads + head], grad[b * C : (b + 1) * C], 0, 0) for b in range(2)
            ]
            back_next = joined * back[1]
            bt1_ref[head] = back_next
            both = back[0] + at(whole, 0, head) * back_next
            scan.up_s[:, i] = both.reshape(NZ, rows, C)
        up_waits.append(
            over_z(
                1 + 2 * len(groups) + g, lambda t, scan=scan: scan.up_s.at[t], scan.up_r
            )
        )

    for head in range(heads):
        attention = att_ref[:, lanes(head)]
        out_cot = o_ref[:, lanes(head)].astype(F32)
        g_s[:, lanes(head)] = jnp.sum(out_cot * attention * inverse, axis=0, keepdims=True)
    gain_wait = over_z(1 + 4 * len(groups), lambda t: g_s, g_r)

    for head in range(heads):
        for block in range(2):
            here = slice(block * C, (block + 1) * C)
            r = block * heads + head
            grad = ag_ref[here, lanes(head)]
            value = v_ref[here, lanes(head)]
            key = k_ref[here, lanes(head)]
            value_part = dot(w_ref[r], grad, 0, 0)
            grad_weights = (dot(grad, value, 1, 1) * mask_ref[r]).astype(BF16)
            key_part = dot(grad_weights, q_ref[here, lanes(head)], 0, 0)
            if block == 0:
                ending = at(to_end, 0, head)
                high, low = split(value.astype(F32) * ending)
                key_part = key_part + dot_split(high, low, bt1_ref[head], 1)
                high, low = split(key.astype(F32) * ending)
                value_part = value_part + dot_split(high, low, bt1_ref[head], 0)
            keyp_ref[here, lanes(head)] = key_part
            valp_ref[here, lanes(head)] = value_part

    down_waits = scan_all(1, up_waits)

    gain_wait()
    row_gain = g_r[0]
    for t in range(1, NZ):
        row_gain = row_gain + g_r[t]
    h_s[...] = row_gain
    over_x(1 + 2 * len(groups), h_s, h_r)()
    gain = h_r[0]
    for r in range(1, nx):
        gain = gain + h_r[r]
    gout[...] = gain.reshape(heads * C)

    for group, scan, arrived in zip(groups, scans[1], down_waits):
        arrived()
        for i, head in enumerate(group):
            came = scan.down_r[:, i].reshape(C, C)
            far = dot_split(ve_ref[0, head], ve_ref[1, head], came, 1)
            kout[:, lanes(head)] = (keyp_ref[:, lanes(head)] + far).astype(BF16)
            far = dot_split(ke_ref[0, head], ke_ref[1, head], came, 0)
            vout[:, lanes(head)] = (valp_ref[:, lanes(head)] + far).astype(BF16)

    for copies in sent:
        copies.wait_send()


def per_device(queries, keys, values, out_grad, log_decay, norm_gain, doc_ids):
    tokens, features = queries.shape
    heads = log_decay.shape[1]
    ndp = lax.axis_size("dp")
    nx = lax.axis_size("seq") // NZ
    rows = C // NZ
    groups = groups_of(heads)
    wide = (tokens, features)
    squares = (2 * heads, C, C)
    halves = (2, heads, tokens, C)
    anywhere = pl.BlockSpec(memory_space=pl.ANY)
    vmem = pltpu.VMEM
    dma = pltpu.SemaphoreType.DMA
    local = (
        (
            vmem(wide, BF16),
            vmem(wide, BF16),
            vmem(wide, BF16),
            vmem(wide, BF16),
            vmem((heads, tokens), F32),
            vmem((1, features), F32),
            pltpu.SMEM((2,), jnp.int32),
        ),
        (
            vmem(squares, F32),
            vmem(squares, BF16),
            vmem((heads, C, C), F32),
            vmem(halves, BF16),
            vmem(squares, BF16),
            vmem(halves, BF16),
            vmem(halves, BF16),
        ),
        (
            vmem(wide, F32),
            vmem(wide, F32),
            vmem(wide, BF16),
            vmem((heads, C, C), F32),
            vmem(wide, F32),
            vmem(wide, F32),
        ),
    )
    info = (
        vmem((1, C), F32),
        vmem((NZ, 1, C), F32),
        vmem((NZ, rows, C), F32),
        vmem((2, NZ, heads, rows, C), F32),
        vmem((2, NZ, heads, rows, C), F32),
        vmem((2, heads, rows, C), F32),
        vmem((1, C), F32),
        vmem((nx, 1, C), F32),
    )

    def scan_of(count):
        table = (NZ, count, rows, C)
        return Scan(
            up_s=vmem(table, F32),
            up_r=vmem(table, F32),
            pre=vmem(table, F32),
            x_s=vmem((count, rows, C), F32),
            x_r=vmem((nx, count, rows, C), F32),
            down_s=vmem(table, F32),
            down_r=vmem(table, F32),
        )

    scans = tuple(tuple(scan_of(len(group)) for group in groups) for _ in range(2))
    norm = (vmem((2, tokens), F32), vmem((ndp, 2, tokens), F32))
    gains = (
        vmem((1, features), F32),
        vmem((NZ, 1, features), F32),
        vmem((1, features), F32),
        vmem((nx, 1, features), F32),
    )
    z_count, x_count = 2 + 4 * len(groups), 2 + 2 * len(groups)
    sems = (
        dma((7,)),
        dma((z_count,)),
        dma((z_count,)),
        dma((x_count,)),
        dma((x_count,)),
        dma,
        dma,
    )
    scratch, tree = jax.tree.flatten((local, info, scans, norm, gains, sems))

    def body(*refs):
        kernel(heads, nx, ndp, refs[:7], refs[7:10], *jax.tree.unflatten(tree, refs[10:]))

    return pl.pallas_call(
        body,
        out_shape=(vmem(wide, BF16), vmem(wide, BF16), vmem((features,), F32)),
        in_specs=[anywhere] * 7,
        out_specs=(pl.BlockSpec(memory_space=pltpu.VMEM),) * 3,
        scratch_shapes=scratch,
        compiler_params=pltpu.CompilerParams(collective_id=0, has_side_effects=True),
        name="attention_core",
    )(queries, keys, values, out_grad, log_decay.T, norm_gain, doc_ids)


def solution(mesh):
    placed = (
        P("seq", "dp"),
        P("seq", "dp"),
        P("seq", "dp"),
        P("seq", "dp"),
        P("seq", "dp"),
        P("dp"),
        P("seq"),
    )
    return jax.shard_map(
        per_device,
        mesh=mesh,
        in_specs=placed,
        out_specs=(P("seq", "dp"), P("seq", "dp"), P("dp")),
        check_vma=False,
    )
```

time: 531 us -> 72.5 us (0.14)
  blocking collectives: 330 us -> 0 us
  waiting for transfers between devices: 89.1 us -> 0 us
  Pallas kernels: 0 us -> 68.9 us
  other arithmetic: 67.4 us -> 0 us
  between operations: 16.3 us -> 0.64 us
  local copies, waits for them, and re-layouts: 12.4 us -> 1.93 us
    unnamed x2 -> x0, blocking collectives: 302 us -> none
    all_gather x2 -> x0, waiting for transfers between devices: 89.1 us -> none  [carried_in(): gathered = jax.tree.map(lambda a: lax.all_gather(a, axis), part)]
    pallas_call x0 -> x1, Pallas kernels: none -> 68.9 us  [per_device(): pl.pallas_call(body, out_shape=(vmem(wide, BF16), vmem(wide, BF16), vmem(...]
    add x67 -> x0, other arithmetic: 65.2 us -> none  [the longest x63 64.8 us: combine_pairs(): later[0][..., None, None] * earlier[1] + later[1]]
    psum x2 -> x0, blocking collectives: 27.5 us -> none  [per_device(): square_total, inner_total = lax.psum((square_part, inner_part), 'dp')]
  transfers between devices with their start and end apart: 3 -> 0, of which waited for: 2 -> 0; matrix products, arithmetic and copies ran while one was open for 1% -> 0% of each run, Pallas kernels for 0% -> 0%
where the time goes in v2:
time: 72.5 us; the launch traced here: 71.5 us
  Pallas kernels  68.9 us (95%)
  local copies, waits for them, and re-layouts  1.93 us (3%)
    pallas_call x1, Pallas kernels, per_device(): pl.pallas_call(body, out_shape=(vmem(wide, BF16), vmem(wide, BF16), vmem(...  68.9 us
    unnamed x3, local copies, waits for them, and re-layouts  1.93 us

profile of v2, /device:TPU:1, one launch (start us, length us, event | category | flops | bytes accessed | tf_op | source)
XLA Modules:
  0.0 71.5 jit_solution(11638230099295534450)
XLA Ops:
  0.6 68.9 %attention_core.1 = (bf16[256,384]{1,0:T(8,128)(2,1)S(1)}, bf16[256,384]{1,0:T(8,128)(2,1)S(1)}, f32[384]{0:T(512)S(1)}) custom-call(bf16[256,384]{1,0:T(8,128)(2,1)} %refs_0_.1, bf16[256,384]{1,0:T(8,128)(2,1)} %refs_1_.1, bf16[256,384]{1,0:T(8,128)(2,1)} %refs_2_.1, bf16[256,384]{1,0:T(8,128)(2,1)} %refs_3_.1, f32[3,256]{1,0:T(4,128)} %bitcast.1, ...), custom_call_target="tpu_custom_call" | custom-call | tf_op jit(solution)/shard_map/attention_core/pallas_call | solution.py:538
  69.6 0.7 copy.13
  70.2 0.6 copy.15
  70.8 0.7 copy.14

commit v3 on v2

--- a/solution.py
+++ b/solution.py
@@ -26,9 +26,10 @@
     return high, (x - high.astype(F32)).astype(BF16)
 
 
-def dot_split(high, low, b, cb):
-    b_high, b_low = split(b)
-    return dot(high, b_high, 1, cb) + (dot(high, b_low, 1, cb) + dot(low, b_high, 1, cb))
+def dot_split(a, b, cb):
+    high, low = split(b)
+    both = dot(a, jnp.concatenate([high, low], axis=1 - cb), 1, cb)
+    return both[:, :C] + both[:, C:]
 
 
 class Scan(NamedTuple):
@@ -47,17 +48,19 @@
 
 def kernel(heads, nx, ndp, ins, outs, local, info, scans, norm, gains, sems):
     q_hbm, k_hbm, v_hbm, o_hbm, log_hbm, gain_hbm, doc_hbm = ins
-    kout, vout, gout = outs
+    gout, k_ref, v_ref, keyp_ref, valp_ref, end_tok_ref, *arriving = outs
     (
-        (q_ref, k_ref, v_ref, o_ref, log_ref, gain_ref, doc_ref),
-        (mask_ref, w_ref, u0_ref, qe_ref, qw_ref, ve_ref, ke_ref),
-        (part_ref, att_ref, ag_ref, bt1_ref, keyp_ref, valp_ref),
+        (q_ref, o_ref, log_ref, gain_ref, doc_ref),
+        (mask_ref, w_ref, u0_ref, qw_ref, open_ref),
+        (part_ref, att_ref, ag_ref, bt1_ref),
     ) = local
     info_s, info_r, keep_ref, step_ref, reach_ref, end_ref, row_s, row_r = info
     st_s, st_r = norm
     g_s, g_r, h_s, h_r = gains
     load_sem, zs_sem, zr_sem, xs_sem, xr_sem, ds_sem, dr_sem = sems
     groups = groups_of(heads)
+    ending_scans = [scan._replace(down_r=r) for scan, r in zip(scans[1], arriving)]
+    scans = (scans[0], ending_scans)
     place = lax.axis_index("seq")
     me = lax.axis_index("dp")
     x = lax.div(place, NZ)
@@ -82,33 +85,17 @@
     for load in loads:
         load.start()
 
-    def each_z(run):
-        def body(i, carry):
-            half = lax.div(i + 1, 2)
-            away = NZ // 2 + half * (1 - 2 * lax.rem(i, 2))
-            run(lax.rem(z + away, NZ))
-            return carry
-
-        lax.fori_loop(0, NZ - 1, body, 0)
-
-    def each_x(run):
-        def body(i, carry):
-            run(lax.rem(x + i, nx))
-            return carry
-
-        lax.fori_loop(1, nx, body, 0)
-
-    def each_dp(run):
-        def body(i, carry):
-            run(lax.rem(me + i, ndp))
-            return carry
-
-        lax.fori_loop(1, ndp, body, 0)
+    aways = [NZ // 2] + [
+        away for near in range(NZ // 2 - 1, 0, -1) for away in (near, NZ - near)
+    ]
+    z_peers = [lax.rem(z + away, NZ) for away in aways]
+    x_peers = [lax.rem(x + away, nx) for away in range(1, nx)]
+    dp_peers = [lax.rem(me + away, ndp) for away in range(1, ndp)]
 
     sent = []
 
-    def exchange(each, where, mine, count, source, slots, send_sem, recv_sem):
-        def start(t):
+    def exchange(peers, where, mine, count, source, slots, send_sem, recv_sem):
+        for t in peers:
             pltpu.make_async_remote_copy(
                 src_ref=source(t),
                 dst_ref=slots.at[mine],
@@ -117,8 +104,6 @@
                 device_id=where(t),
                 device_id_type=MESH,
             ).start()
-
-        each(start)
         slots[mine] = source(mine)[...]
         others = slots.at[pl.ds(0, count - 1)]
         whole = pltpu.make_async_remote_copy(
@@ -134,7 +119,7 @@
 
     def over_z(phase, source, slots):
         return exchange(
-            each_z,
+            z_peers,
             lambda t: {"seq": x * NZ + t},
             z,
             NZ,
@@ -146,7 +131,7 @@
 
     def over_x(phase, source, slots):
         return exchange(
-            each_x,
+            x_peers,
             lambda t: {"seq": t * NZ + z},
             x,
             nx,
@@ -161,9 +146,12 @@
     def greet(**where):
         pl.semaphore_signal(barrier, inc=1, device_id=where, device_id_type=MESH)
 
-    each_z(lambda t: greet(seq=x * NZ + t))
-    each_x(lambda t: greet(seq=t * NZ + z))
-    each_dp(lambda t: greet(dp=t))
+    for t in z_peers:
+        greet(seq=x * NZ + t)
+    for t in x_peers:
+        greet(seq=t * NZ + z)
+    for t in dp_peers:
+        greet(dp=t)
 
     for load in loads[:2]:
         load.wait()
@@ -217,44 +205,6 @@
         over_z(1 + g, lambda t, scan=scan: scan.up_s.at[t], scan.up_r)
         for g, scan in enumerate(scans[0])
     ]
-
-    info_wait()
-
-    def tile(line, i):
-        return jnp.broadcast_to(line[:, i : i + 1], (rows, C))
-
-    def goes_on(later, earlier):
-        return jnp.where(
-            later[:, heads : heads + 1] == earlier[:, heads + 1 : heads + 2], 1.0, 0.0
-        )
-
-    line = info_r[0]
-    reach = jnp.ones((1, C), F32)
-    for t in range(NZ):
-        if t:
-            earlier, line = line, info_r[t]
-            keeps = goes_on(line, earlier)
-            keep_ref[t] = jnp.broadcast_to(keeps, (rows, C))
-            for head in range(heads):
-                step_ref[0, t, head] = tile(keeps * earlier, head)
-                step_ref[1, t, head] = tile(keeps * line, head)
-            reach = reach * (keeps * earlier)
-        for head in range(heads):
-            reach_ref[0, t, head] = tile(reach, head)
-    first, last = info_r[0], info_r[NZ - 1]
-    row_s[...] = jnp.where(
-        lane < heads, reach * last, jnp.where(lane == heads, first, last)
-    )
-    row_wait = over_x(0, row_s, row_r)
-    for head in range(heads):
-        end_ref[0, head] = tile(last, head)
-        end_ref[1, head] = tile(first, head)
-    reach = jnp.ones((1, C), F32)
-    for t in range(NZ - 1, -1, -1):
-        for head in range(heads):
-            reach_ref[1, t, head] = tile(reach, head)
-        if t:
-            reach = reach * (goes_on(info_r[t], info_r[t - 1]) * info_r[t])
 
     for load in loads[4:]:
         load.wait()
@@ -271,27 +221,51 @@
             weights = (dot(query, key, 1, 1) * mask).astype(BF16)
             w_ref[r] = weights
             near = dot(weights, value, 1, 0)
-            weighted = query.astype(F32) * at(from_start, block, head)
-            qw_ref[r] = weighted.astype(BF16)
+            opening = at(from_start, block, head)
+            qw_ref[r] = (query.astype(F32) * opening).astype(BF16).T
             if block == 1:
-                high, low = split(weighted * joined)
-                near = near + dot_split(high, low, u0_ref[head], 0)
-                weighted = weighted * (joined * at(whole, 0, head))
-            high, low = split(weighted)
-            qe_ref[0, head, here] = high
-            qe_ref[1, head, here] = low
+                near = near + (joined * opening) * dot_split(query, u0_ref[head], 0)
+                opening = opening * (joined * at(whole, 0, head))
             part_ref[here, lanes(head)] = near
             ending = at(to_end, block, head)
             if block == 0:
                 ending = ending * (joined * at(whole, 1, head))
-            high, low = split(value.astype(F32) * ending)
-            ve_ref[0, head, here] = high
-            ve_ref[1, head, here] = low
-            high, low = split(key.astype(F32) * ending)
-            ke_ref[0, head, here] = high
-            ke_ref[1, head, here] = low
-    row_wait()
-    row_lines = [row_r[r] for r in range(nx)]
+            open_ref[here, head : head + 1] = opening
+            end_tok_ref[here, head : head + 1] = ending
+
+    info_wait()
+
+    def tile(line, i):
+        return jnp.broadcast_to(line[:, i : i + 1], (rows, C))
+
+    def goes_on(later, earlier):
+        return jnp.where(
+            later[:, heads : heads + 1] == earlier[:, heads + 1 : heads + 2], 1.0, 0.0
+        )
+
+    line = info_r[0]
+    reach = jnp.ones((1, C), F32)
+    for t in range(NZ):
+        if t:
+            earlier, line = line, info_r[t]
+            keeps = goes_on(line, earlier)
+            keep_ref[t] = jnp.broadcast_to(keeps, (rows, C))
+            for head in range(heads):
+                step_ref[0, t, head] = tile(keeps * earlier, head)
+            reach = reach * (keeps * earlier)
+        for head in range(heads):
+            reach_ref[0, t, head] = tile(reach, head)
+    first, last = info_r[0], info_r[NZ - 1]
+    row_s[...] = jnp.where(
+        lane < heads, reach * last, jnp.where(lane == heads, first, last)
+    )
+    row_wait = over_x(0, row_s, row_r)
+    for head in range(heads):
+        end_ref[0, head] = tile(last, head)
+        end_ref[1, head] = tile(first, head)
+
+    def row_lines_of():
+        return [row_r[r] for r in range(nx)]
 
     def scan_row(back, scan, group):
         count = len(group)
@@ -312,6 +286,7 @@
 
     def scan_rows(back, scan, group):
         count = len(group)
+        row_lines = row_lines_of()
         entering = [jnp.zeros((rows, C), F32)] * count
         chosen = entering
         for r in range(nx - 2, -1, -1) if back else range(1, nx):
@@ -327,6 +302,16 @@
             for i, head in enumerate(group):
                 scan.down_s[t, i] = scan.pre[t, i] + reach_ref[back, t, head] * chosen[i]
 
+    def back_factors():
+        reach = jnp.ones((1, C), F32)
+        for t in range(NZ - 1, -1, -1):
+            for head in range(heads):
+                reach_ref[1, t, head] = tile(reach, head)
+                if t:
+                    step_ref[1, t, head] = keep_ref[t] * tile(info_r[t], head)
+            if t:
+                reach = reach * (goes_on(info_r[t], info_r[t - 1]) * info_r[t])
+
     def scan_all(back, up_waits):
         base = 1 + back * 2 * len(groups)
         x_waits, down_waits = [], []
@@ -334,6 +319,8 @@
             up_waits[g]()
             scan_row(back, scan, group)
             x_waits.append(over_x(1 + back * len(groups) + g, scan.x_s, scan.x_r))
+        if not back:
+            row_wait()
         for g, (group, scan) in enumerate(zip(groups, scans[back])):
             x_waits[g]()
             scan_rows(back, scan, group)
@@ -345,6 +332,7 @@
         return down_waits
 
     down_waits = scan_all(0, up_waits)
+    back_factors()
 
     squares = jnp.zeros((tokens, C), F32)
     inners = jnp.zeros((tokens, C), F32)
@@ -352,20 +340,17 @@
         arrived()
         for i, head in enumerate(group):
             came = scan.down_r[:, i].reshape(C, C)
-            far = dot_split(qe_ref[0, head], qe_ref[1, head], came, 0)
-            attention = part_ref[:, lanes(head)] + far
+            far = dot_split(q_ref[:, lanes(head)], came, 0)
+            attention = part_ref[:, lanes(head)] + open_ref[:, head : head + 1] * far
             att_ref[:, lanes(head)] = attention
             wanted = o_ref[:, lanes(head)].astype(F32) * gain_ref[:, lanes(head)]
             squares = squares + attention * attention
             inners = inners + wanted * attention
-    lane = lax.broadcasted_iota(jnp.int32, (tokens, C), 1)
-    stats = jnp.where(
-        lane == 0,
-        jnp.sum(squares, axis=1, keepdims=True),
-        jnp.sum(inners, axis=1, keepdims=True),
-    ).T
-    st_s[...] = stats[0:2]
-    exchange(each_dp, lambda t: {"dp": t}, me, ndp, lambda t: st_s, st_r, ds_sem, dr_sem)()
+    ones = jnp.ones((8, 2 * C), BF16)
+    for i, summed in enumerate((squares, inners)):
+        halves = jnp.concatenate(split(summed), axis=1)
+        st_s[i : i + 1] = dot(ones, halves, 1, 1)[0:1]
+    exchange(dp_peers, lambda t: {"dp": t}, me, ndp, lambda t: st_s, st_r, ds_sem, dr_sem)()
     sums = st_r[0]
     for r in range(1, ndp):
         sums = sums + st_r[r]
@@ -385,7 +370,7 @@
             grad = ((wanted - attention * bend) * inverse).astype(BF16)
             ag_ref[:, lanes(head)] = grad
             back = [
-                dot(qw_ref[b * heads + head], grad[b * C : (b + 1) * C], 0, 0) for b in range(2)
+                dot(qw_ref[b * heads + head], grad[b * C : (b + 1) * C], 1, 0) for b in range(2)
             ]
             back_next = joined * back[1]
             bt1_ref[head] = back_next
@@ -415,10 +400,8 @@
             key_part = dot(grad_weights, q_ref[here, lanes(head)], 0, 0)
             if block == 0:
                 ending = at(to_end, 0, head)
-                high, low = split(value.astype(F32) * ending)
-                key_part = key_part + dot_split(high, low, bt1_ref[head], 1)
-                high, low = split(key.astype(F32) * ending)
-                value_part = value_part + dot_split(high, low, bt1_ref[head], 0)
+                key_part = key_part + ending * dot_split(value, bt1_ref[head], 1)
+                value_part = value_part + ending * dot_split(key, bt1_ref[head], 0)
             keyp_ref[here, lanes(head)] = key_part
             valp_ref[here, lanes(head)] = value_part
 
@@ -435,17 +418,35 @@
         gain = gain + h_r[r]
     gout[...] = gain.reshape(heads * C)
 
-    for group, scan, arrived in zip(groups, scans[1], down_waits):
+    for arrived in down_waits:
         arrived()
-        for i, head in enumerate(group):
-            came = scan.down_r[:, i].reshape(C, C)
-            far = dot_split(ve_ref[0, head], ve_ref[1, head], came, 1)
-            kout[:, lanes(head)] = (keyp_ref[:, lanes(head)] + far).astype(BF16)
-            far = dot_split(ke_ref[0, head], ke_ref[1, head], came, 0)
-            vout[:, lanes(head)] = (valp_ref[:, lanes(head)] + far).astype(BF16)
-
     for copies in sent:
         copies.wait_send()
+
+
+def finish(heads, ins, outs, scratch):
+    gain_ref, k_ref, v_ref, keyp_ref, valp_ref, end_tok_ref, *arriving = ins
+    kout_hbm, vout_hbm, gout_hbm = outs
+    kout, vout, sem = scratch
+    stores = [pltpu.make_async_copy(gain_ref, gout_hbm, sem.at[2 * heads])]
+    stores[0].start()
+    for group, down_r in zip(groups_of(heads), arriving):
+        for i, head in enumerate(group):
+            lanes = slice(head * C, (head + 1) * C)
+            came = down_r[:, i].reshape(C, C)
+            ending = end_tok_ref[:, head : head + 1]
+            far = ending * dot_split(v_ref[:, lanes], came, 1)
+            kout[:, lanes] = (keyp_ref[:, lanes] + far).astype(BF16)
+            far = ending * dot_split(k_ref[:, lanes], came, 0)
+            vout[:, lanes] = (valp_ref[:, lanes] + far).astype(BF16)
+            for j, (src, dst) in enumerate(((kout, kout_hbm), (vout, vout_hbm))):
+                store = pltpu.make_async_copy(
+                    src.at[:, lanes], dst.at[:, lanes], sem.at[2 * head + j]
+                )
+                store.start()
+                stores.append(store)
+    for store in stores:
+        store.wait()
 
 
 def per_device(queries, keys, values, out_grad, log_decay, norm_gain, doc_ids):
@@ -457,14 +458,11 @@
     groups = groups_of(heads)
     wide = (tokens, features)
     squares = (2 * heads, C, C)
-    halves = (2, heads, tokens, C)
     anywhere = pl.BlockSpec(memory_space=pl.ANY)
     vmem = pltpu.VMEM
     dma = pltpu.SemaphoreType.DMA
     local = (
         (
-            vmem(wide, BF16),
-            vmem(wide, BF16),
             vmem(wide, BF16),
             vmem(wide, BF16),
             vmem((heads, tokens), F32),
@@ -475,18 +473,14 @@
             vmem(squares, F32),
             vmem(squares, BF16),
             vmem((heads, C, C), F32),
-            vmem(halves, BF16),
             vmem(squares, BF16),
-            vmem(halves, BF16),
-            vmem(halves, BF16),
+            vmem((tokens, heads), F32),
         ),
         (
             vmem(wide, F32),
             vmem(wide, F32),
             vmem(wide, BF16),
             vmem((heads, C, C), F32),
-            vmem(wide, F32),
-            vmem(wide, F32),
         ),
     )
     info = (
@@ -530,20 +524,45 @@
         dma,
         dma,
     )
+    between = (
+        vmem((features,), F32),
+        vmem(wide, BF16),
+        vmem(wide, BF16),
+        vmem(wide, F32),
+        vmem(wide, F32),
+        vmem((tokens, heads), F32),
+    ) + tuple(vmem((NZ, len(group), rows, C), F32) for group in groups)
     scratch, tree = jax.tree.flatten((local, info, scans, norm, gains, sems))
 
     def body(*refs):
-        kernel(heads, nx, ndp, refs[:7], refs[7:10], *jax.tree.unflatten(tree, refs[10:]))
-
-    return pl.pallas_call(
+        ins, outs, rest = refs[:7], refs[7 : 7 + len(between)], refs[7 + len(between) :]
+        kernel(heads, nx, ndp, ins, outs, *jax.tree.unflatten(tree, rest))
+
+    def last(*refs):
+        finish(heads, refs[: len(between)], refs[len(between) :][:3], refs[len(between) + 3 :])
+
+    inside = pl.BlockSpec(memory_space=pltpu.VMEM)
+    held = pl.pallas_call(
         body,
-        out_shape=(vmem(wide, BF16), vmem(wide, BF16), vmem((features,), F32)),
+        out_shape=between,
         in_specs=[anywhere] * 7,
-        out_specs=(pl.BlockSpec(memory_space=pltpu.VMEM),) * 3,
+        out_specs=(inside,) * len(between),
         scratch_shapes=scratch,
         compiler_params=pltpu.CompilerParams(collective_id=0, has_side_effects=True),
         name="attention_core",
     )(queries, keys, values, out_grad, log_decay.T, norm_gain, doc_ids)
+    return pl.pallas_call(
+        last,
+        out_shape=(
+            jax.ShapeDtypeStruct(wide, BF16),
+            jax.ShapeDtypeStruct(wide, BF16),
+            jax.ShapeDtypeStruct((features,), F32),
+        ),
+        in_specs=[inside] * len(between),
+        out_specs=(anywhere,) * 3,
+        scratch_shapes=[vmem(wide, BF16), vmem(wide, BF16), dma((2 * heads + 1,))],
+        name="outputs",
+    )(*(pltpu.with_memory_space_constraint(part, pltpu.VMEM) for part in held))
 
 
 def solution(mesh):

time: 72.5 us -> 69.7 us (0.961); the launches traced: 71.5 us -> 69.6 us
  local copies, waits for them, and re-layouts: 1.93 us -> 0 us
    unnamed x3 -> x0, local copies, waits for them, and re-layouts: 1.93 us -> none
    pallas_call x1 -> x2, Pallas kernels: 68.9 us -> 68.9 us  [the longest x1 67.8 us: per_device(): pl.pallas_call(body, out_shape=between, in_specs=[anywhere] * 7, out_spec...]
where the time goes in v3:
time: 69.7 us; the launch traced here: 69.6 us
  Pallas kernels  68.9 us (99%)
    pallas_call x1, Pallas kernels, per_device(): pl.pallas_call(body, out_shape=between, in_specs=[anywhere] * 7, out_spec...  67.8 us

profile of v3, /device:TPU:1, one launch (start us, length us, event | category | flops | bytes accessed | tf_op | source)
XLA Modules:
  0.0 69.6 jit_solution(5443242034635723057)
XLA Ops:
  0.6 67.8 %attention_core.1 = (f32[384]{0:T(512)S(1)}, bf16[256,384]{1,0:T(8,128)(2,1)S(1)}, bf16[256,384]{1,0:T(8,128)(2,1)S(1)}, f32[256,384]{1,0:T(8,128)S(1)}, f32[256...) custom-call(bf16[256,384]{1,0:T(8,128)(2,1)} %refs_0_.1, ...), custom_call_target="tpu_custom_call" | custom-call | tf_op jit(solution)/shard_map/attention_core/pallas_call | solution.py:545
  68.5 1.1 %outputs.1 = (bf16[256,384]{1,0:T(8,128)(2,1)}, bf16[256,384]{1,0:T(8,128)(2,1)}, f32[384]{0:T(512)}) custom-call(f32[384]{0:T(512)S(1)} %get-tuple-element.11.refs_0_, bf16[256,384]{1,0:T(8,128)(2,1)S(1)} %get-tuple-element.12.refs_1_, bf16[256,384]{1,0:T(8,128)(2,1)S(1)} %get-tuple-element.13.refs_2_, f32[256,384]{1,0:T(8,128)S(1)} %get-tuple-element.14.refs_3_, ...), custom_call_target="tpu_custom_call" | custom-call | tf_op jit(solution)/shard_map/outputs/pallas_call | solution.py:554

commit v4 on v3

--- a/solution.py
+++ b/solution.py
@@ -68,6 +68,25 @@
     rows = C // NZ
     tokens = 2 * C
 
+    def aways(count):
+        return sorted(range(1, count), key=lambda away: (-min(away, count - away), -away))
+
+    z_peers = [lax.rem(z + away, NZ) for away in aways(NZ)]
+    x_peers = [lax.rem(x + away, nx) for away in aways(nx)]
+    dp_peers = [lax.rem(me + away, ndp) for away in aways(ndp)]
+
+    barrier = pltpu.get_barrier_semaphore()
+
+    def greet(**where):
+        pl.semaphore_signal(barrier, inc=1, device_id=where, device_id_type=MESH)
+
+    for t in z_peers:
+        greet(seq=x * NZ + t)
+    for t in x_peers:
+        greet(seq=t * NZ + z)
+    for t in dp_peers:
+        greet(dp=t)
+
     loads = [
         pltpu.make_async_copy(src, dst, load_sem.at[i])
         for i, (src, dst) in enumerate(
@@ -84,13 +103,6 @@
     ]
     for load in loads:
         load.start()
-
-    aways = [NZ // 2] + [
-        away for near in range(NZ // 2 - 1, 0, -1) for away in (near, NZ - near)
-    ]
-    z_peers = [lax.rem(z + away, NZ) for away in aways]
-    x_peers = [lax.rem(x + away, nx) for away in range(1, nx)]
-    dp_peers = [lax.rem(me + away, ndp) for away in range(1, ndp)]
 
     sent = []
 
@@ -140,18 +152,6 @@
             xs_sem.at[phase],
             xr_sem.at[phase],
         )
-
-    barrier = pltpu.get_barrier_semaphore()
-
-    def greet(**where):
-        pl.semaphore_signal(barrier, inc=1, device_id=where, device_id_type=MESH)
-
-    for t in z_peers:
-        greet(seq=x * NZ + t)
-    for t in x_peers:
-        greet(seq=t * NZ + z)
-    for t in dp_peers:
-        greet(dp=t)
 
     for load in loads[:2]:
         load.wait()

time: 69.7 us -> 69.8 us (level)
  no operation moved by 1% of the time
where the time goes in v4:
time: 69.8 us; the launch traced here: 69.3 us
  Pallas kernels  68.7 us (98%)
    pallas_call x1, Pallas kernels, per_device(): pl.pallas_call(body, out_shape=between, in_specs=[anywhere] * 7, out_spec...  67.6 us

profile of v4, /device:TPU:1, one launch (start us, length us, event | category | flops | bytes accessed | tf_op | source)
XLA Modules:
  0.0 69.3 jit_solution(1760344685009120798)
XLA Ops:
  0.6 67.6 %attention_core.1 = (f32[384]{0:T(512)S(1)}, bf16[256,384]{1,0:T(8,128)(2,1)S(1)}, bf16[256,384]{1,0:T(8,128)(2,1)S(1)}, f32[256,384]{1,0:T(8,128)S(1)}, f32[256...) custom-call(bf16[256,384]{1,0:T(8,128)(2,1)} %refs_0_.1, ...), custom_call_target="tpu_custom_call" | custom-call | tf_op jit(solution)/shard_map/attention_core/pallas_call | solution.py:545
  68.3 1.1 %outputs.1 = (bf16[256,384]{1,0:T(8,128)(2,1)}, bf16[256,384]{1,0:T(8,128)(2,1)}, f32[384]{0:T(512)}) custom-call(f32[384]{0:T(512)S(1)} %get-tuple-element.11.refs_0_, bf16[256,384]{1,0:T(8,128)(2,1)S(1)} %get-tuple-element.12.refs_1_, bf16[256,384]{1,0:T(8,128)(2,1)S(1)} %get-tuple-element.13.refs_2_, f32[256,384]{1,0:T(8,128)S(1)} %get-tuple-element.14.refs_3_, ...), custom_call_target="tpu_custom_call" | custom-call | tf_op jit(solution)/shard_map/outputs/pallas_call | solution.py:554

commit v5 on v4

--- a/solution.py
+++ b/solution.py
@@ -54,7 +54,7 @@
         (mask_ref, w_ref, u0_ref, qw_ref, open_ref),
         (part_ref, att_ref, ag_ref, bt1_ref),
     ) = local
-    info_s, info_r, keep_ref, step_ref, reach_ref, end_ref, row_s, row_r = info
+    keep_ref, step_ref, reach_ref, end_ref, row_s, row_r = info
     st_s, st_r = norm
     g_s, g_r, h_s, h_r = gains
     load_sem, zs_sem, zr_sem, xs_sem, xr_sem, ds_sem, dr_sem = sems
@@ -107,17 +107,19 @@
     sent = []
 
     def exchange(peers, where, mine, count, source, slots, send_sem, recv_sem):
+        used = pl.ds(0, source(mine).shape[0])
+
         for t in peers:
             pltpu.make_async_remote_copy(
                 src_ref=source(t),
-                dst_ref=slots.at[mine],
+                dst_ref=slots.at[mine, used],
                 send_sem=send_sem,
                 recv_sem=recv_sem,
                 device_id=where(t),
                 device_id_type=MESH,
             ).start()
-        slots[mine] = source(mine)[...]
-        others = slots.at[pl.ds(0, count - 1)]
+        slots[mine, used] = source(mine)[...]
+        others = slots.at[pl.ds(0, count - 1), used]
         whole = pltpu.make_async_remote_copy(
             src_ref=others,
             dst_ref=others,
@@ -184,7 +186,8 @@
     for i in range(2):
         document = jnp.full((1, C), doc_ref[i], jnp.int32).astype(F32)
         line = jnp.where(lane == heads + i, document, line)
-    info_s[...] = line
+    for t in range(NZ):
+        scans[0][0].up_s[t, len(groups[0]) * rows : len(groups[0]) * rows + 1] = line
 
     for load in loads[2:4]:
         load.wait()
@@ -197,13 +200,18 @@
                 updates.append(dot(scaled.astype(BF16), v_ref[here, lanes(head)], 0, 0))
             u0_ref[head] = updates[0]
             both = (joined * at(whole, 1, head)) * updates[0] + updates[1]
-            scan.up_s[:, i] = both.reshape(NZ, rows, C)
+            scan.up_s[:, i * rows : (i + 1) * rows] = both.reshape(NZ, rows, C)
 
     pl.semaphore_wait(barrier, (NZ - 1) + (nx - 1) + (ndp - 1))
-    info_wait = over_z(0, lambda t: info_s, info_r)
     up_waits = [
-        over_z(1 + g, lambda t, scan=scan: scan.up_s.at[t], scan.up_r)
-        for g, scan in enumerate(scans[0])
+        over_z(
+            1 + g,
+            lambda t, scan=scan, used=len(group) * rows + (g == 0): scan.up_s.at[
+                t, pl.ds(0, used)
+            ],
+            scan.up_r,
+        )
+        for g, (group, scan) in enumerate(zip(groups, scans[0]))
     ]
 
     for load in loads[4:]:
@@ -233,7 +241,11 @@
             open_ref[here, head : head + 1] = opening
             end_tok_ref[here, head : head + 1] = ending
 
-    info_wait()
+    up_waits[0]()
+
+    def info_of(t):
+        row = len(groups[0]) * rows
+        return scans[0][0].up_r[t, row : row + 1]
 
     def tile(line, i):
         return jnp.broadcast_to(line[:, i : i + 1], (rows, C))
@@ -243,11 +255,11 @@
             later[:, heads : heads + 1] == earlier[:, heads + 1 : heads + 2], 1.0, 0.0
         )
 
-    line = info_r[0]
+    line = info_of(0)
     reach = jnp.ones((1, C), F32)
     for t in range(NZ):
         if t:
-            earlier, line = line, info_r[t]
+            earlier, line = line, info_of(t)
             keeps = goes_on(line, earlier)
             keep_ref[t] = jnp.broadcast_to(keeps, (rows, C))
             for head in range(heads):
@@ -255,7 +267,7 @@
             reach = reach * (keeps * earlier)
         for head in range(heads):
             reach_ref[0, t, head] = tile(reach, head)
-    first, last = info_r[0], info_r[NZ - 1]
+    first, last = info_of(0), info_of(NZ - 1)
     row_s[...] = jnp.where(
         lane < heads, reach * last, jnp.where(lane == heads, first, last)
     )
@@ -277,12 +289,14 @@
             if t != order[-1]:
                 link = t if back else t + 1
                 state = [
-                    step_ref[back, link, head] * state[i] + keep_ref[link] * scan.up_r[t, i]
+                    step_ref[back, link, head] * state[i] + keep_ref[link] * scan.up_r[t, i * rows : (i + 1) * rows]
                     for i, head in enumerate(group)
                 ]
             else:
                 for i, head in enumerate(group):
-                    scan.x_s[i] = end_ref[back, head] * state[i] + scan.up_r[t, i]
+                    scan.x_s[i] = end_ref[back, head] * state[i] + scan.up_r[
+                        t, i * rows : (i + 1) * rows
+                    ]
 
     def scan_rows(back, scan, group):
         count = len(group)
@@ -308,15 +322,16 @@
             for head in range(heads):
                 reach_ref[1, t, head] = tile(reach, head)
                 if t:
-                    step_ref[1, t, head] = keep_ref[t] * tile(info_r[t], head)
+                    step_ref[1, t, head] = keep_ref[t] * tile(info_of(t), head)
             if t:
-                reach = reach * (goes_on(info_r[t], info_r[t - 1]) * info_r[t])
+                reach = reach * (goes_on(info_of(t), info_of(t - 1)) * info_of(t))
 
     def scan_all(back, up_waits):
         base = 1 + back * 2 * len(groups)
         x_waits, down_waits = [], []
         for g, (group, scan) in enumerate(zip(groups, scans[back])):
-            up_waits[g]()
+            if back or g:
+                up_waits[g]()
             scan_row(back, scan, group)
             x_waits.append(over_x(1 + back * len(groups) + g, scan.x_s, scan.x_r))
         if not back:
@@ -375,7 +390,7 @@
             back_next = joined * back[1]
             bt1_ref[head] = back_next
             both = back[0] + at(whole, 0, head) * back_next
-            scan.up_s[:, i] = both.reshape(NZ, rows, C)
+            scan.up_s[:, i * rows : (i + 1) * rows] = both.reshape(NZ, rows, C)
         up_waits.append(
             over_z(
                 1 + 2 * len(groups) + g, lambda t, scan=scan: scan.up_s.at[t], scan.up_r
@@ -484,8 +499,6 @@
         ),
     )
     info = (
-        vmem((1, C), F32),
-        vmem((NZ, 1, C), F32),
         vmem((NZ, rows, C), F32),
         vmem((2, NZ, heads, rows, C), F32),
         vmem((2, NZ, heads, rows, C), F32),
@@ -494,11 +507,12 @@
         vmem((nx, 1, C), F32),
     )
 
-    def scan_of(count):
+    def scan_of(count, extra):
         table = (NZ, count, rows, C)
+        taken = (NZ, count * rows + extra, C)
         return Scan(
-            up_s=vmem(table, F32),
-            up_r=vmem(table, F32),
+            up_s=vmem(taken, F32),
+            up_r=vmem(taken, F32),
             pre=vmem(table, F32),
             x_s=vmem((count, rows, C), F32),
             x_r=vmem((nx, count, rows, C), F32),
@@ -506,7 +520,12 @@
             down_r=vmem(table, F32),
         )
 
-    scans = tuple(tuple(scan_of(len(group)) for group in groups) for _ in range(2))
+    scans = tuple(
+        tuple(
+            scan_of(len(group), 8 if back == g == 0 else 0) for g, group in enumerate(groups)
+        )
+        for back in range(2)
+    )
     norm = (vmem((2, tokens), F32), vmem((ndp, 2, tokens), F32))
     gains = (
         vmem((1, features), F32),

time: 69.8 us -> 69.3 us (level)
  Pallas kernels: 68.7 us -> 67.7 us
    pallas_call x1, Pallas kernels: 67.6 us -> 66.6 us  [per_device(): pl.pallas_call(body, out_shape=between, in_specs=[anywhere] * 7, out_spec...]
where the time goes in v5:
time: 69.3 us; the launch traced here: 68.4 us
  Pallas kernels  67.7 us (98%)
    pallas_call x1, Pallas kernels, per_device(): pl.pallas_call(body, out_shape=between, in_specs=[anywhere] * 7, out_spec...  66.6 us

profile of v5, /device:TPU:1, one launch (start us, length us, event | category | flops | bytes accessed | tf_op | source)
XLA Modules:
  0.0 68.4 jit_solution(9645212241271917474)
XLA Ops:
  0.6 66.6 %attention_core.1 = (f32[384]{0:T(512)S(1)}, bf16[256,384]{1,0:T(8,128)(2,1)S(1)}, bf16[256,384]{1,0:T(8,128)(2,1)S(1)}, f32[256,384]{1,0:T(8,128)S(1)}, f32[256...) custom-call(bf16[256,384]{1,0:T(8,128)(2,1)} %refs_0_.1, ...), custom_call_target="tpu_custom_call" | custom-call | tf_op jit(solution)/shard_map/attention_core/pallas_call | solution.py:564
  67.3 1.1 %outputs.1 = (bf16[256,384]{1,0:T(8,128)(2,1)}, bf16[256,384]{1,0:T(8,128)(2,1)}, f32[384]{0:T(512)}) custom-call(f32[384]{0:T(512)S(1)} %get-tuple-element.11.refs_0_, bf16[256,384]{1,0:T(8,128)(2,1)S(1)} %get-tuple-element.12.refs_1_, bf16[256,384]{1,0:T(8,128)(2,1)S(1)} %get-tuple-element.13.refs_2_, f32[256,384]{1,0:T(8,128)S(1)} %get-tuple-element.14.refs_3_, ...), custom_call_target="tpu_custom_call" | custom-call | tf_op jit(solution)/shard_map/outputs/pallas_call | solution.py:573
